TPU v7x, 256 devices: a whole 4x4x8 slice. The times are simulated.
256 devices in a mesh: gy: 8 (over z), gz: 32 (over y, x, core).
Axes of the slice: x: 4, y: 4, z: 8, core: 2. Of those that a mesh axis runs over, the one named last changes fastest.
Arguments:
- scalar: float32 [1024, 512, 128], P('gz', 'gy'), may hold values from -6 to 6
- velocity: bfloat16 [3, 1024, 512, 128], P(None, 'gz', 'gy'), may hold values from -4 to 4
- row_shift: int32 [1024], P('gz'), may hold values from 0 to 32, as said below
- frac_index: int32 [1024], P('gz'), may hold values from 0 to 7
- brick_rank: int32 [32], replicated, may hold values from 0 to 31, each once
- color_coeffs: float32 [3, 4], replicated, may hold values from -1 to 1
- extinction: float32 [2], replicated, may hold values from 0.5 to 2
Outputs:
- field: float32 [1024, 512, 128], P('gz', 'gy')
- image: float32 [4, 512, 128], P(None, 'gy', 'gz')
Inputs may be any that keep to these rules, and one draw needn't show every extreme that they name: `row_shift`: some slice is shifted by exactly 32 rows in every draw. `brick_rank`: a permutation of the brick indices.
All inputs are finite; a program needn't handle non-finite values.
Results may differ from a plain program's by a relative error of at most 0.0003.
Values may be sent and summed in bfloat16 or wider, within the bound.
No kernel may reach another device: no remote copies, remote signals or barrier semaphores. Data moves between devices by JAX's collectives and lax.ppermute only.
A program may use at most 64 MiB of HBM per device.

v0:
```python
import jax
import jax.numpy as jnp
from jax import lax
from jax.sharding import PartitionSpec as P

NFRAC = 8
SHIFT_MAX = 32


diffusivity = 0.05
time_step = 0.2


def with_halo(cells, sides, width):
    for axis, dim in sides:
        count = lax.axis_size(axis)
        ends = count - 1
        head = lax.slice_in_dim(cells, 0, width, axis=dim)
        tail = lax.slice_in_dim(cells, cells.shape[dim] - width, cells.shape[dim], axis=dim)
        cells = jnp.concatenate(
            [
                lax.ppermute(tail, axis, [(i, (i + 1) % count) for i in range(ends)]),
                cells,
                lax.ppermute(head, axis, [((i + 1) % count, i) for i in range(ends)]),
            ],
            axis=dim,
        )
    return cells


def passed_along(value, axis, by):
    count = lax.axis_size(axis)
    pairs = [(i, i + by) for i in range(count) if 0 <= i + by < count]
    return lax.ppermute(value, axis, pairs)


def tendency(padded, velocity):
    wide = jnp.pad(padded, ((0, 0), (0, 0), (1, 1)))
    centre = wide[1:-1, 1:-1, 1:-1]
    z_next = wide[2:, 1:-1, 1:-1]
    z_prev = wide[:-2, 1:-1, 1:-1]
    y_next = wide[1:-1, 2:, 1:-1]
    y_prev = wide[1:-1, :-2, 1:-1]
    x_next = wide[1:-1, 1:-1, 2:]
    x_prev = wide[1:-1, 1:-1, :-2]
    flow = velocity.astype(jnp.float32)
    advection = 0.5 * (
        flow[0] * (z_next - z_prev) + flow[1] * (y_next - y_prev) + flow[2] * (x_next - x_prev)
    )
    laplacian = z_next + z_prev + y_next + y_prev + x_next + x_prev - 6.0 * centre
    return diffusivity * laplacian - advection


def trimmed(values, margin):
    return values[margin : values.shape[0] - margin, margin : values.shape[1] - margin]


def inside(depth_cells, rows, width):
    z_index = (
        lax.axis_index("gz") * depth_cells
        - width
        + jnp.arange(depth_cells + 2 * width, dtype=jnp.int32)
    )
    y_index = lax.axis_index("gy") * rows - width + jnp.arange(rows + 2 * width, dtype=jnp.int32)
    z_valid = (z_index >= 0) & (z_index < depth_cells * lax.axis_size("gz"))
    y_valid = (y_index >= 0) & (y_index < rows * lax.axis_size("gy"))
    return (z_valid[:, None] & y_valid[None, :]).astype(jnp.float32)[:, :, None]


def shear_slices(joined, row_shift, frac_index, margin, height):
    fraction = frac_index.astype(jnp.float32) / NFRAC

    def one_slice(slab, offset, weight):
        start = margin + 1 - offset
        nearer = lax.dynamic_slice_in_dim(slab, start, height, 0)
        farther = lax.dynamic_slice_in_dim(slab, start - 1, height, 0)
        return (1.0 - weight) * nearer + weight * farther

    return jax.vmap(one_slice)(joined, row_shift, fraction)


def brick_light(values, color_coeffs, extinction, slice_depth):
    channels = []
    for colour_index in range(3):
        coeffs = color_coeffs[colour_index]
        channels.append(
            coeffs[0] + values * (coeffs[1] + values * (coeffs[2] + values * coeffs[3]))
        )
    emission = jnp.stack(channels, 0)
    optical = (extinction[0] * values * values + extinction[1]) * slice_depth
    before = jnp.cumsum(optical, axis=0) - optical
    weights = jnp.exp(-before) * (1.0 - jnp.exp(-optical))
    colour = jnp.sum(weights[None] * emission, axis=1)
    depth = jnp.sum(optical, axis=0)
    return (colour, depth)


def composite(colour, depth, brick_rank):
    precede = (brick_rank[:, None] < brick_rank[None, :]).astype(jnp.float32)
    earlier = jnp.einsum("jk,jyx->kyx", precede, depth, precision=lax.Precision.HIGHEST)
    shaded = jnp.sum(jnp.exp(-earlier)[:, None] * colour, axis=0)
    opacity = 1.0 - jnp.exp(-jnp.sum(depth, axis=0))
    return jnp.concatenate([shaded, opacity[None]], 0)


def on_device(scalar, velocity, row_shift, frac_index, brick_rank, color_coeffs, extinction):
    depth_cells, rows, columns = scalar.shape
    padded = with_halo(scalar, (("gy", 1), ("gz", 0)), 3)
    flow = with_halo(velocity, (("gy", 2), ("gz", 1)), 2)

    def flow_trim(margin):
        return flow[:, margin : flow.shape[1] - margin, margin : flow.shape[2] - margin]

    first = trimmed(padded, 1) + time_step * tendency(padded, flow_trim(0))
    first = first * inside(depth_cells, rows, 2)
    second = 0.75 * trimmed(padded, 2) + 0.25 * (
        trimmed(first, 1) + time_step * tendency(first, flow_trim(1))
    )
    second = second * inside(depth_cells, rows, 1)
    field = 1.0 / 3.0 * trimmed(padded, 3) + 2.0 / 3.0 * (
        trimmed(second, 1) + time_step * tendency(second, flow_trim(2))
    )
    margin = SHIFT_MAX
    top_rows = field[:, rows - margin - 1 :, :]
    above = passed_along(top_rows, "gy", 1)
    joined = jnp.concatenate([above, field], 1)
    sheared = shear_slices(joined, row_shift, frac_index, margin, rows)
    slice_depth = 1.0 / (depth_cells * lax.axis_size("gz"))
    colour, depth = brick_light(sheared, color_coeffs, extinction, slice_depth)
    stacked = jnp.concatenate([colour, depth[None]], 0)[None]
    blocks = lax.all_to_all(stacked, "gz", split_axis=3, concat_axis=0, tiled=True)
    image = composite(blocks[:, :3], blocks[:, 3], brick_rank)
    return (field, image)


def solution(mesh):
    placed = (P("gz", "gy", None), P(None, "gz", "gy", None), P("gz"), P("gz"), P(), P(), P())
    return jax.shard_map(
        on_device,
        mesh=mesh,
        in_specs=placed,
        out_specs=(P("gz", "gy", None), P(None, "gy", "gz")),
        check_vma=False,
    )
```

profile of v0, /device:TPU:129, one launch (start us, length us, event | category | flops | bytes accessed | tf_op | source)
XLA Modules:
  0.0 103.3 jit_solution(10348414686183695718)
XLA Ops:
  0.6 1.1 %fusion.55 = (bf16[3,32,2,128]{3,2,1,0:T(2,128)(2,1)S(1)}, bf16[3,32,2,128]{3,2,1,0:T(2,128)(2,1)S(1)}) fusion(bf16[3,32,64,128]{3,2,1,0:T(8,128)(2,1)} %param.8), kind=kLoop, calls=%fused_computation.112 | loop fusion | bytes 196608 | tf_op jit(solution)/shard_map/slice | solution.py:18
  1.8 2.6 %collective-permute-start.4 = (bf16[3,32,2,128]{3,1,2,0:T(8,128)(2,1)S(1)}, bf16[3,32,2,128]{3,1,2,0:T(8,128)(2,1)S(1)}, u32[]{:S(2)}, u32[]{:S(2)}) collective-permute-start(bf16[3,32,2,128]{3,1,2,0:T(8,128)(2,1)S(1)} %copy.76), channel_id=1, source_target_pairs={{0,32},{32,64},{64,96},{96,128},{128,160},{160,192},{192,224},{1,3... | collective-permute-start | bytes 147464 | tf_op jit(solution)/shard_map/ppermute | solution.py:22
  4.4 3.8 %collective-permute-start.5 = (bf16[3,32,2,128]{3,1,2,0:T(8,128)(2,1)S(1)}, bf16[3,32,2,128]{3,1,2,0:T(8,128)(2,1)S(1)}, u32[]{:S(2)}, u32[]{:S(2)}) collective-permute-start(bf16[3,32,2,128]{3,1,2,0:T(8,128)(2,1)S(1)} %copy.77), channel_id=1, source_target_pairs={{32,0},{64,32},{96,64},{128,96},{160,128},{192,160},{224,192},{33,... | collective-permute-start | bytes 147464 | tf_op jit(solution)/shard_map/ppermute | solution.py:24
  8.3 1.0 fusion.57
  9.3 1.9 %collective-permute-start = (f32[32,3,128]{2,0,1:T(8,128)S(1)}, f32[32,3,128]{2,0,1:T(8,128)S(1)}, u32[]{:S(2)}, u32[]{:S(2)}) collective-permute-start(f32[32,3,128]{2,0,1:T(8,128)S(1)} %copy.78), channel_id=1, source_target_pairs={{0,32},{32,64},{64,96},{96,128},{128,160},{160,192},{192,224},{1,3... | collective-permute-start | bytes 147464 | tf_op jit(solution)/shard_map/ppermute | solution.py:22
  11.2 4.6 %collective-permute-start.1 = (f32[32,3,128]{2,0,1:T(8,128)S(1)}, f32[32,3,128]{2,0,1:T(8,128)S(1)}, u32[]{:S(2)}, u32[]{:S(2)}) collective-permute-start(f32[32,3,128]{2,0,1:T(8,128)S(1)} %copy.79), channel_id=1, source_target_pairs={{32,0},{64,32},{96,64},{128,96},{160,128},{192,160},{224,192},{33,... | collective-permute-start | bytes 147464 | tf_op jit(solution)/shard_map/ppermute | solution.py:24
  16.0 1.8 %fusion.58 = (f32[1,1]{1,0:T(1,128)}, f32[1,1]{1,0:T(1,128)}, f32[1,1]{1,0:T(1,128)}, f32[1,1]{1,0:T(1,128)}, f32[1,1]{1,0:T(1,128)}, /*index=5*/f32[1,1]{1,0:T(...) fusion(f32[3,4]{1,0:T(4,128)} %param.12), kind=kLoop, calls=%fused_computation.115 | loop fusion | bytes 96 | tf_op jit(solution)/shard_map/slice | solution.py:87
  17.9 2.7 %constant_dynamic-update-slice_fusion.4 = (bf16[3,32,68,128]{3,1,2,0:T(8,128)(2,1)S(1)}, f32[3,32,64,128]{3,1,2,0:T(8,128)S(1)}) fusion(bf16[3,32,68,128]{3,1,2,0:T(8,128)(2,1)S(1)} %constant_dynamic-update-slice_fusion.5, bf16[3,32,64,128]{3,2,1,0:T(8,128)(2,1)} %param.8), kind=kLoop, calls=%fused_computation.87 | loop fusion | flops 786432 | bytes 6291456
  20.8 4.8 %collective-permute-start.6 = (bf16[3,2,68,128]{3,1,2,0:T(2,128)(2,1)S(1)}, bf16[3,2,68,128]{3,1,2,0:T(2,128)(2,1)S(1)}, u32[]{:S(2)}, u32[]{:S(2)}) collective-permute-start(bf16[3,2,68,128]{3,1,2,0:T(2,128)(2,1)S(1)} %get-tuple-element.12), channel_id=1, source_target_pairs={{0,1},{1,2},{2,3},{3,4},{4,5},{5,6},{6,7},{7,8},{8,9},{9,10},{10,1... | collective-permute-start | bytes 313352 | tf_op jit(solution)/shard_map/ppermute | solution.py:22
  25.6 1.9 %collective-permute-start.7 = (bf16[3,2,68,128]{3,1,2,0:T(2,128)(2,1)S(1)}, bf16[3,2,68,128]{3,1,2,0:T(2,128)(2,1)S(1)}, u32[]{:S(2)}, u32[]{:S(2)}) collective-permute-start(bf16[3,2,68,128]{3,1,2,0:T(2,128)(2,1)S(1)} %get-tuple-element.13), channel_id=1, source_target_pairs={{1,0},{2,1},{3,2},{4,3},{5,4},{6,5},{7,6},{8,7},{9,8},{10,9},{11,1... | collective-permute-start | bytes 313352 | tf_op jit(solution)/shard_map/ppermute | solution.py:24
  28.2 3.6 %collective-permute-start.2 = (f32[3,70,128]{2,0,1:T(4,128)S(1)}, f32[3,70,128]{2,0,1:T(4,128)S(1)}, u32[]{:S(2)}, u32[]{:S(2)}) collective-permute-start(f32[3,70,128]{2,0,1:T(4,128)S(1)} %get-tuple-element.18), channel_id=1, source_target_pairs={{0,1},{1,2},{2,3},{3,4},{4,5},{5,6},{6,7},{7,8},{8,9},{9,10},{10,1... | collective-permute-start | bytes 322568 | tf_op jit(solution)/shard_map/ppermute | solution.py:22
  31.9 1.9 %collective-permute-start.3 = (f32[3,70,128]{2,0,1:T(4,128)S(1)}, f32[3,70,128]{2,0,1:T(4,128)S(1)}, u32[]{:S(2)}, u32[]{:S(2)}) collective-permute-start(f32[3,70,128]{2,0,1:T(4,128)S(1)} %get-tuple-element.19), channel_id=1, source_target_pairs={{1,0},{2,1},{3,2},{4,3},{5,4},{6,5},{7,6},{8,7},{9,8},{10,9},{11,1... | collective-permute-start | bytes 322568 | tf_op jit(solution)/shard_map/ppermute | solution.py:24
  33.8 1.2 %fusion.52 = (f32[3,36,68,128]{3,1,2,0:T(8,128)S(1)}, bf16[3,36,68,128]{3,1,2,0:T(8,128)(2,1)S(1)}) fusion(bf16[3,2,68,128]{3,1,2,0:T(2,128)(2,1)S(1)} %collective-permute-done.7, bf16[3,32,68,128]{3,1,2,0:T(8,128)(2,1)S(1)} %constant_dynamic-update-slice_fusion.3, bf16[3,2,68,128]{3,1,2,0:T(2,128)(2,1)S(1)} %collective-permute-done.6), kind=kLoop, calls=%fused_computation.110 | loop fusion | flops 6580224 | bytes 7520256 | tf_op jit(solution)/shard_map/convert_element_type | solution.py:46
  35.1 0.9 slice_convert_fusion
  35.9 2.4 %collective-permute-done.3 = f32[3,70,128]{2,0,1:T(4,128)S(1)} collective-permute-done((f32[3,70,128]{2,0,1:T(4,128)S(1)}, f32[3,70,128]{2,0,1:T(4,128)S(1)}, u32[]{:S(2)}, u32[]{:S(2)}) %collective-permute-start.3) | collective-permute-done | bytes 107552 | tf_op jit(solution)/shard_map/ppermute | solution.py:24
  38.5 1.9 %fusion.7 = f32[36,68,128]{2,0,1:T(8,128)S(1)} fusion(f32[3,36,68,128]{3,1,2,0:T(8,128)S(1)} %get-tuple-element.10, f32[38,70,128]{2,0,1:T(8,128)S(1)} %pad_maximum_fusion.2, f32[36,68]{0,1:T(8,128)S(1)} %and_convert_fusion.1), kind=kLoop, calls=%fused_computation.22 | loop fusion | flops 6580224 | bytes 13864960 | tf_op jit(solution)/shard_map/mul | solution.py:115
  40.4 2.0 %fusion.19 = f32[34,66,128]{2,0,1:T(8,128)S(1)} fusion(f32[3,34,66,128]{3,1,2,0:T(8,128)S(1)} %slice_convert_fusion, f32[38,70,128]{2,0,1:T(8,128)S(1)} %pad_maximum_fusion.2, f32[36,68,128]{2,0,1:T(8,128)S(1)} %fusion.7, f32[34,66]{0,1:T(8,128)S(1)} %and_convert_fusion), kind=kLoop, calls=%fused_computation.37 | loop fusion | flops 6893568 | bytes 14743552 | tf_op jit(solution)/shard_map/mul | solution.py:119
  42.5 1.5 %fusion.33 = f32[32,64,128]{2,0,1:T(8,128)S(1)} fusion(f32[3,32,64,128]{3,1,2,0:T(8,128)S(1)} %get-tuple-element.17, f32[34,66,128]{2,0,1:T(8,128)S(1)} %fusion.19, f32[32,64,128]{2,1,0:T(8,128)S(1)} %copy-done.3), kind=kLoop, calls=%fused_computation.56 | loop fusion | flops 6029312 | bytes 11837440 | tf_op jit(solution)/shard_map/add | solution.py:120
  44.0 2.1 %collective-permute-start.8 = (f32[32,33,128]{2,0,1:T(8,128)S(1)}, f32[32,33,128]{2,0,1:T(8,128)S(1)}, u32[]{:S(2)}, u32[]{:S(2)}) collective-permute-start(f32[32,33,128]{2,0,1:T(8,128)S(1)} %slice.317), channel_id=1, source_target_pairs={{0,32},{32,64},{64,96},{96,128},{128,160},{160,192},{192,224},{1,3... | collective-permute-start | bytes 1622024 | tf_op jit(solution)/shard_map/ppermute | solution.py:34
  46.8 11.7 %collective-permute-done.8 = f32[32,33,128]{2,0,1:T(8,128)S(1)} collective-permute-done((f32[32,33,128]{2,0,1:T(8,128)S(1)}, f32[32,33,128]{2,0,1:T(8,128)S(1)}, u32[]{:S(2)}, u32[]{:S(2)}) %collective-permute-start.8) | collective-permute-done | bytes 540704 | tf_op jit(solution)/shard_map/ppermute | solution.py:34
  58.6 2.8 %gather_fusion = f32[32,64,128]{2,0,1:T(8,128)S(1)} fusion(f32[32,97,128]{2,0,1:T(8,128)S(1)} %pad_maximum_fusion.1, s32[32]{0:T(128)S(1)} %get-tuple-element.40), kind=kCustom, calls=%fused_computation | custom fusion | bytes 2097536 | tf_op jit(solution)/shard_map/vmap()/gather | solution.py:75
  61.4 3.7 %gather_fusion.1 = f32[32,64,128]{2,0,1:T(8,128)} fusion(f32[32,97,128]{2,0,1:T(8,128)S(1)} %pad_maximum_fusion.1, s32[32]{0:T(128)S(1)} %get-tuple-element.41), kind=kCustom, calls=%fused_computation.1 | custom fusion | bytes 2097536 | tf_op jit(solution)/shard_map/vmap()/gather | solution.py:76
  65.1 5.2 %subtract_multiply_fusion = f32[32,64,128]{2,1,0:T(8,128)S(1)} fusion(f32[]{:T(128)} %bitcast.15, f32[32,64,128]{2,0,1:T(8,128)} %gather_fusion.1, f32[32]{0:T(128)S(1)} %get-tuple-element.39, f32[32,64,128]{2,0,1:T(8,128)S(1)} %gather_fusion, f32[32]{0:T(128)S(1)} %get-tuple-element.38, f32[]{:T(128)} %bitcast.10), kind=kOutput, calls=%fused_computation.71 | output fusion | flops 13107200 | bytes 3145992 | tf_op jit(solution)/shard_map/jit(cumsum)/reduce_window_sum | solution.py:91
  70.3 2.6 %fusion.50 = f32[64,128]{1,0:T(8,128)S(1)} fusion(f32[]{:T(128)} %bitcast.15, f32[32,64,128]{2,0,1:T(8,128)S(1)} %copy-done, f32[32]{0:T(128)S(1)} %get-tuple-element.39, f32[32,64,128]{2,0,1:T(8,128)S(1)} %gather_fusion, f32[32]{0:T(128)S(1)} %get-tuple-element.38, f32[]{:T(128)} %bitcast.10), kind=kLoop, calls=%fused_computation.109 | loop fusion | flops 2088960 | bytes 2130184 | tf_op jit(solution)/shard_map/reduce_sum | solution.py:94
  73.5 2.9 %multiply_add_fusion.2 = (f32[1,32,64,128]{3,1,2,0:T(8,128)S(1)}, f32[1,32,64,128]{3,1,2,0:T(8,128)S(1)}) fusion(f32[]{:T(128)} %bitcast.21, f32[]{:T(128)} %bitcast.20, f32[]{:T(128)} %bitcast.19, f32[]{:T(128)} %bitcast.16, f32[32,64,128]{2,0,1:T(8,128)S(1)} %copy-done, f32[32]{0:T(128)S(1)} %get-tuple-element.39, f32[32,64,128]{2,0,1:T(8,128)S(1)} %gather_fusion, ...), kind=kLoop, calls=%fused_computation.70 | loop fusion | flops 2359296 | bytes 4194576 | tf_op jit(solution)/shard_map/add | solution.py:87
  76.4 5.5 %multiply_add_fusion.1 = (f32[1,32,64,128]{3,1,2,0:T(8,128)S(1)}, f32[1,32,64,128]{3,1,2,0:T(8,128)S(1)}) fusion(f32[1,32,64,128]{3,1,2,0:T(8,128)S(1)} %get-tuple-element.9, f32[]{:T(128)} %bitcast.25, f32[]{:T(128)} %bitcast.24, f32[]{:T(128)} %bitcast.23, f32[]{:T(128)} %bitcast.22, f32[]{:T(128)} %bitcast.29, f32[]{:T(128)} %bitcast.28, f32[]{:T(128)} %bitcast.27, ...), kind=kLoop, calls=%fused_computation.69 | loop fusion | flops 3145728 | bytes 3145760 | tf_op jit(solution)/shard_map/add | solution.py:87
  81.9 0.8 fusion
  82.9 0.9 reshape.272
  83.8 9.2 %all-to-all-start = ((f32[32,1,1024]{2,1,0:T(1,128)}), f32[32,1,1024]{2,1,0:T(1,128)S(1)}, u32[]{:S(2)}, u32[]{:S(2)}) async-start(f32[32,1,1024]{2,1,0:T(1,128)} %reshape.272), calls=%async_computation | async-start | bytes 262144 | tf_op jit(solution)/shard_map/all_to_all | solution.py:131
  93.0 1.6 %copy.48 = f32[32,64,128]{2,1,0:T(8,128)} copy(f32[32,64,128]{2,0,1:T(8,128)S(1)} %copy-done.2) | data formatting | bytes 2097152
  94.6 6.0 %all-to-all-done = f32[32,1,1024]{2,1,0:T(1,128)S(1)} async-done(((f32[32,1,1024]{2,1,0:T(1,128)}), f32[32,1,1024]{2,1,0:T(1,128)S(1)}, u32[]{:S(2)}, u32[]{:S(2)}) %all-to-all-start) | async-done | bytes 131104 | tf_op jit(solution)/shard_map/all_to_all | solution.py:131
  101.1 0.9 reduce.1
  (57 shorter events, 4.6 us)
Async XLA Ops:
  1.8 16.1 %collective-permute-start.4 = (bf16[3,32,2,128]{3,1,2,0:T(8,128)(2,1)S(1)}, bf16[3,32,2,128]{3,1,2,0:T(8,128)(2,1)S(1)}, u32[]{:S(2)}, u32[]{:S(2)}) collective-permute-start(bf16[3,32,2,128]{3,1,2,0:T(8,128)(2,1)S(1)} %copy.76), channel_id=1, source_target_pairs={{0,32},{32,64},{64,96},{96,128},{128,160},{160,192},{192,224},{1,3... | collective-permute-start | bytes 147464 | tf_op jit(solution)/shard_map/ppermute | solution.py:22
  4.4 16.1 %collective-permute-start.5 = (bf16[3,32,2,128]{3,1,2,0:T(8,128)(2,1)S(1)}, bf16[3,32,2,128]{3,1,2,0:T(8,128)(2,1)S(1)}, u32[]{:S(2)}, u32[]{:S(2)}) collective-permute-start(bf16[3,32,2,128]{3,1,2,0:T(8,128)(2,1)S(1)} %copy.77), channel_id=1, source_target_pairs={{32,0},{64,32},{96,64},{128,96},{160,128},{192,160},{224,192},{33,... | collective-permute-start | bytes 147464 | tf_op jit(solution)/shard_map/ppermute | solution.py:24
  9.3 18.2 %collective-permute-start = (f32[32,3,128]{2,0,1:T(8,128)S(1)}, f32[32,3,128]{2,0,1:T(8,128)S(1)}, u32[]{:S(2)}, u32[]{:S(2)}) collective-permute-start(f32[32,3,128]{2,0,1:T(8,128)S(1)} %copy.78), channel_id=1, source_target_pairs={{0,32},{32,64},{64,96},{96,128},{128,160},{160,192},{192,224},{1,3... | collective-permute-start | bytes 147464 | tf_op jit(solution)/shard_map/ppermute | solution.py:22
  11.2 16.9 %collective-permute-start.1 = (f32[32,3,128]{2,0,1:T(8,128)S(1)}, f32[32,3,128]{2,0,1:T(8,128)S(1)}, u32[]{:S(2)}, u32[]{:S(2)}) collective-permute-start(f32[32,3,128]{2,0,1:T(8,128)S(1)} %copy.79), channel_id=1, source_target_pairs={{32,0},{64,32},{96,64},{128,96},{160,128},{192,160},{224,192},{33,... | collective-permute-start | bytes 147464 | tf_op jit(solution)/shard_map/ppermute | solution.py:24
  17.9 9.7 %copy-start.3 = (f32[32,64,128]{2,1,0:T(8,128)S(1)}, f32[32,64,128]{2,1,0:T(8,128)}, u32[]{:S(2)}) copy-start(f32[32,64,128]{2,1,0:T(8,128)} %param.7) | copy-start | bytes 3145732
  20.8 13.1 %collective-permute-start.6 = (bf16[3,2,68,128]{3,1,2,0:T(2,128)(2,1)S(1)}, bf16[3,2,68,128]{3,1,2,0:T(2,128)(2,1)S(1)}, u32[]{:S(2)}, u32[]{:S(2)}) collective-permute-start(bf16[3,2,68,128]{3,1,2,0:T(2,128)(2,1)S(1)} %get-tuple-element.12), channel_id=1, source_target_pairs={{0,1},{1,2},{2,3},{3,4},{4,5},{5,6},{6,7},{7,8},{8,9},{9,10},{10,1... | collective-permute-start | bytes 313352 | tf_op jit(solution)/shard_map/ppermute | solution.py:22
  25.6 8.3 %collective-permute-start.7 = (bf16[3,2,68,128]{3,1,2,0:T(2,128)(2,1)S(1)}, bf16[3,2,68,128]{3,1,2,0:T(2,128)(2,1)S(1)}, u32[]{:S(2)}, u32[]{:S(2)}) collective-permute-start(bf16[3,2,68,128]{3,1,2,0:T(2,128)(2,1)S(1)} %get-tuple-element.13), channel_id=1, source_target_pairs={{1,0},{2,1},{3,2},{4,3},{5,4},{6,5},{7,6},{8,7},{9,8},{10,9},{11,1... | collective-permute-start | bytes 313352 | tf_op jit(solution)/shard_map/ppermute | solution.py:24
  28.2 7.7 %collective-permute-start.2 = (f32[3,70,128]{2,0,1:T(4,128)S(1)}, f32[3,70,128]{2,0,1:T(4,128)S(1)}, u32[]{:S(2)}, u32[]{:S(2)}) collective-permute-start(f32[3,70,128]{2,0,1:T(4,128)S(1)} %get-tuple-element.18), channel_id=1, source_target_pairs={{0,1},{1,2},{2,3},{3,4},{4,5},{5,6},{6,7},{7,8},{8,9},{9,10},{10,1... | collective-permute-start | bytes 322568 | tf_op jit(solution)/shard_map/ppermute | solution.py:22
  31.9 6.4 %collective-permute-start.3 = (f32[3,70,128]{2,0,1:T(4,128)S(1)}, f32[3,70,128]{2,0,1:T(4,128)S(1)}, u32[]{:S(2)}, u32[]{:S(2)}) collective-permute-start(f32[3,70,128]{2,0,1:T(4,128)S(1)} %get-tuple-element.19), channel_id=1, source_target_pairs={{1,0},{2,1},{3,2},{4,3},{5,4},{6,5},{7,6},{8,7},{9,8},{10,9},{11,1... | collective-permute-start | bytes 322568 | tf_op jit(solution)/shard_map/ppermute | solution.py:24
  42.4 3.7 %copy-start.5 = (f32[2]{0:T(128)S(1)}, f32[2]{0:T(128)}, u32[]{:S(2)}) copy-start(f32[2]{0:T(128)} %param.13) | copy-start | bytes 28
  42.5 4.3 %copy-start.6 = (s32[32]{0:T(128)S(1)}, s32[32]{0:T(128)}, u32[]{:S(2)}) copy-start(s32[32]{0:T(128)} %param.9) | copy-start | bytes 388
  42.5 4.3 %copy-start.7 = (s32[32]{0:T(128)S(1)}, s32[32]{0:T(128)}, u32[]{:S(2)}) copy-start(s32[32]{0:T(128)} %param.10) | copy-start | bytes 388
  44.0 14.6 %copy-start.1 = (f32[32,64,128]{2,0,1:T(8,128)}, f32[32,64,128]{2,0,1:T(8,128)S(1)}, u32[]{:S(2)}) copy-start(f32[32,64,128]{2,0,1:T(8,128)S(1)} %fusion.33) | copy-start | bytes 3145732
  44.0 14.4 %collective-permute-start.8 = (f32[32,33,128]{2,0,1:T(8,128)S(1)}, f32[32,33,128]{2,0,1:T(8,128)S(1)}, u32[]{:S(2)}, u32[]{:S(2)}) collective-permute-start(f32[32,33,128]{2,0,1:T(8,128)S(1)} %slice.317), channel_id=1, source_target_pairs={{0,32},{32,64},{64,96},{96,128},{128,160},{160,192},{192,224},{1,3... | collective-permute-start | bytes 1622024 | tf_op jit(solution)/shard_map/ppermute | solution.py:34
  65.1 5.2 %copy-start = (f32[32,64,128]{2,0,1:T(8,128)S(1)}, f32[32,64,128]{2,0,1:T(8,128)}, u32[]{:S(2)}) copy-start(f32[32,64,128]{2,0,1:T(8,128)} %gather_fusion.1) | copy-start | bytes 3145732
  82.7 10.3 %copy-start.2 = (f32[32,64,128]{2,0,1:T(8,128)S(1)}, f32[32,64,128]{2,0,1:T(8,128)}, u32[]{:S(2)}) copy-start(f32[32,64,128]{2,0,1:T(8,128)} %copy-done.1) | copy-start | bytes 3145732
  83.8 16.8 %all-to-all-start = ((f32[32,1,1024]{2,1,0:T(1,128)}), f32[32,1,1024]{2,1,0:T(1,128)S(1)}, u32[]{:S(2)}, u32[]{:S(2)}) async-start(f32[32,1,1024]{2,1,0:T(1,128)} %reshape.272), calls=%async_computation | async-start | bytes 262144 | tf_op jit(solution)/shard_map/all_to_all | solution.py:131
  93.0 9.4 %copy-start.4 = (s32[32]{0:T(128)S(1)}, s32[32]{0:T(128)}, u32[]{:S(2)}) copy-start(s32[32]{0:T(128)} %param.11) | copy-start | bytes 388
where the time goes:
time: 104 us; the launch traced here: 103 us
  starting transfers between devices  36.6 us (35%)
  other arithmetic  29.2 us (28%)
  waiting for transfers between devices  20.1 us (19%)
  local copies, waits for them, and re-layouts  16 us (15%)
  between operations  1.14 us (1%)
    ppermute x4, starting transfers between devices, with_halo(): lax.ppermute(tail, axis, [(i, (i + 1) % count) for i in range(ends)])  13 us
    ppermute x4, starting transfers between devices, with_halo(): lax.ppermute(head, axis, [((i + 1) % count, i) for i in range(ends)])  12.3 us
    ppermute x1, waiting for transfers between devices, passed_along(): return lax.ppermute(value, axis, pairs)  11.7 us
    all_to_all x1, starting transfers between devices, on_device(): lax.all_to_all(stacked, 'gz', split_axis=3, concat_axis=0, tiled=True)  9.2 us
    add x2, other arithmetic, brick_light(): coeffs[0] + values * (coeffs[1] + values * (coeffs[2] + values * coeffs[3]))  8.33 us
    all_to_all x1, waiting for transfers between devices, on_device(): lax.all_to_all(stacked, 'gz', split_axis=3, concat_axis=0, tiled=True)  6 us
    another operation x1, other arithmetic, brick_light(): before = jnp.cumsum(optical, axis=0) - optical  5.19 us
    gather x1, local copies, waits for them, and re-layouts, one_slice(): farther = lax.dynamic_slice_in_dim(slab, start - 1, height, 0)  3.72 us
  transfers between devices with their start and end apart: 10, of which 3 were waited for; matrix products, arithmetic and copies ran while one was open for 10% of the time, Pallas kernels for 0%

commit v1 on v0

v1 whole, which is shorter than its diff:
```python
import jax
import jax.numpy as jnp
import numpy as np
from jax import lax
from jax.experimental import pallas as pl
from jax.experimental.pallas import tpu as pltpu
from jax.sharding import PartitionSpec as P

NFRAC = 8
SHIFT_MAX = 32
CZ, CY, CX = 32, 64, 128
PZ = 40
PLANE = CY
SS_ROWS = PZ * PLANE + 16
UU_PLANE = PZ * PLANE
TOP = SHIFT_MAX + 1
SH_ROWS = CZ * TOP
F32, BF16, I16 = jnp.float32, jnp.bfloat16, jnp.int16
VM = pl.BlockSpec(memory_space=pltpu.VMEM)
SM = pl.BlockSpec(memory_space=pltpu.SMEM)


def params():
    return pltpu.CompilerParams(vmem_limit_bytes=24 * 1024 * 1024)


def call(kernel, outs, n_smem, n_vmem, scratch=(), aliases=None, cost=(1000000, 1000000)):
    return pl.pallas_call(
        kernel,
        out_shape=outs,
        in_specs=[SM] * n_smem + [VM] * n_vmem,
        out_specs=jax.tree.map(lambda _: VM, outs),
        scratch_shapes=list(scratch),
        input_output_aliases=aliases or {},
        compiler_params=params(),
        cost_estimate=pl.CostEstimate(flops=cost[0], bytes_accessed=cost[1], transcendentals=0),
    )


def shaped(shape, dtype):
    return jax.ShapeDtypeStruct(shape, dtype)


def shifted(value, axis, by):
    count = lax.axis_size(axis)
    pairs = [(i, i + by) for i in range(count) if 0 <= i + by < count]
    return lax.ppermute(value, axis, pairs)


def split(value):
    high = value.astype(BF16)
    return high, (value - high.astype(F32)).astype(BF16)


def pack_z(s_ref, u_ref, up_ref, down_ref):
    for out, s_lo, u_lo in ((up_ref, CZ - 3, CZ - 2), (down_ref, 0, 0)):
        high, low = split(s_ref[s_lo : s_lo + 3].reshape(3 * CY, CX))
        out[0 : 3 * CY] = high
        out[3 * CY : 6 * CY] = low
        for comp in range(3):
            out[(6 + 2 * comp) * CY : (8 + 2 * comp) * CY] = u_ref[comp, u_lo : u_lo + 2].reshape(2 * CY, CX)


def flat(z):
    return 8 + PLANE * (z + 4)


def assemble(s_ref, u_ref, below_ref, above_ref, ss_ref, uu_ref, up_ref, down_ref, face):
    ss_ref[0:8] = jnp.zeros((8, CX), F32)
    ss_ref[SS_ROWS - 8 : SS_ROWS] = jnp.zeros((8, CX), F32)
    for z in (-4, CZ + 3):
        ss_ref[flat(z) : flat(z) + CY] = jnp.zeros((CY, CX), F32)
    for halo, z in ((below_ref, -3), (above_ref, CZ)):
        ss_ref[flat(z) : flat(z) + 3 * CY] = halo[0 : 3 * CY].astype(F32) + halo[3 * CY : 6 * CY].astype(F32)

    def copy_plane(z, _):
        base = pl.multiple_of(flat(z), 8)
        ss_ref[pl.ds(base, CY)] = s_ref[z]
        for comp in range(3):
            base = pl.multiple_of(comp * UU_PLANE + PLANE * (z + 4), 8)
            uu_ref[pl.ds(base, CY)] = u_ref[comp, z].astype(F32)
        return 0

    lax.fori_loop(0, CZ, copy_plane, 0, unroll=2)
    for comp in range(3):
        for halo, z in ((below_ref, -2), (above_ref, CZ)):
            base = comp * UU_PLANE + PLANE * (z + 4)
            uu_ref[base : base + 2 * CY] = halo[(6 + 2 * comp) * CY : (8 + 2 * comp) * CY].astype(F32)
        for z in (-4, -3, CZ + 2, CZ + 3):
            base = comp * UU_PLANE + PLANE * (z + 4)
            uu_ref[base : base + CY] = jnp.zeros((CY, CX), F32)
    for out, s_lo, u_lo in ((up_ref, CY - 3, CY - 2), (down_ref, 0, 0)):
        for row in range(3):
            value = ss_ref[pl.ds(8 + s_lo + row, PZ, stride=PLANE)]
            high = value.astype(BF16).astype(F32)
            face[row * PZ : (row + 1) * PZ] = high
            face[(3 + row) * PZ : (4 + row) * PZ] = value - high
        for comp in range(3):
            for row in range(2):
                at = 6 + 2 * comp + row
                face[at * PZ : (at + 1) * PZ] = uu_ref[pl.ds(comp * UU_PLANE + u_lo + row, PZ, stride=PLANE)]
        out[...] = face[...].astype(BF16)


def advance(c, zn, zp, yn, yp, uz, uy, ux, lane):
    rows = c.shape[0]
    xn = jnp.where(lane == CX - 1, 0.0, pltpu.roll(c, CX - 1, 1))
    xp = jnp.where(lane == 0, 0.0, pltpu.roll(c, 1, 1))
    total = (zn + zp) + (yn + yp) + (xn + xp)
    flow = uz * (zn - zp) + uy * (yn - yp) + ux * (xn - xp)
    return 0.94 * c + (0.01 * total - 0.1 * flow)


CHUNK = 16


def stencil(edge_ref, ss_ref, uu_ref, field_ref, f1, f2):
    lane = lax.broadcasted_iota(jnp.int32, (CHUNK, CX), 1)

    def sweep(src, z_lo, z_hi, put):
        def plane(z, _):
            base = pl.multiple_of(flat(z), 8)
            near = src.at[pl.ds(pl.multiple_of(base - 8, 8), CY + 16)]
            after = src.at[pl.ds(pl.multiple_of(base + PLANE, 8), CY)]
            before = src.at[pl.ds(pl.multiple_of(base - PLANE, 8), CY)]
            vel = [uu_ref.at[pl.ds(pl.multiple_of(comp * UU_PLANE + base - 8, 8), CY)] for comp in range(3)]
            for k in range(0, CY, CHUNK):
                here = slice(k, k + CHUNK)
                value = advance(
                    near[8 + k : 8 + k + CHUNK],
                    after[here],
                    before[here],
                    near[9 + k : 9 + k + CHUNK],
                    near[7 + k : 7 + k + CHUNK],
                    *[v[here] for v in vel],
                    lane,
                )
                put(z, base, k, value)
            return 0

        lax.fori_loop(z_lo, z_hi, plane, 0, unroll=2)

    def put_first(z, base, k, value):
        f1[pl.ds(pl.multiple_of(base + k, 8), CHUNK)] = value

    def put_second(z, base, k, value):
        at = pl.multiple_of(base + k, 8)
        f2[pl.ds(at, CHUNK)] = 0.75 * ss_ref[pl.ds(at, CHUNK)] + 0.25 * value

    def put_field(z, base, k, value):
        at = pl.multiple_of(base + k, 8)
        field_ref[z, pl.ds(k, CHUNK), :] = (1.0 / 3.0) * ss_ref[pl.ds(at, CHUNK)] + (2.0 / 3.0) * value

    def mask(dst, width):
        for z, side in ((-width, 0), (CZ, 1)):
            rows = slice(flat(z), flat(z) + width * CY)
            dst[rows] = dst[rows] * edge_ref[side]

    sweep(ss_ref, -2, CZ + 2, put_first)
    mask(f1, 2)
    sweep(f1, -1, CZ + 1, put_second)
    mask(f2, 1)
    sweep(f2, 0, CZ, put_field)


def powers_of_two():
    return jnp.asarray((2.0 ** (np.arange(128) - 110.0)).astype(np.float32).reshape(1, 128))


def edges(edge_ref, pow_ref, ss_ref, uu_ref, below_ref, above_ref, old_ref, field_ref, shear_ref, face, se, ue, fe, ge, top):
    lane = lax.broadcasted_iota(jnp.int32, (PZ, CX), 1)
    spot = lax.broadcasted_iota(jnp.int32, (PZ, CX), 0)
    z_mask = jnp.where(spot < 4, edge_ref[0], jnp.where(spot >= 4 + CZ, edge_ref[1], 1.0))
    field_ref[...] = old_ref[...]

    def at(row):
        return 8 + row * PZ

    for side in (0, 1):
        halo = (below_ref, above_ref)[side]
        face[...] = halo[...].astype(F32)
        own = range(0, 6) if side == 0 else range(CY - 6, CY)
        first_own = 3 if side == 0 else 0
        first_halo = 0 if side == 0 else 6
        for n, y in enumerate(own):
            r = at(first_own + n)
            se[r : r + PZ] = ss_ref[pl.ds(8 + y, PZ, stride=PLANE)]
        for n in range(3):
            r = at(first_halo + n)
            se[r : r + PZ] = face[n * PZ : (n + 1) * PZ] + face[(3 + n) * PZ : (4 + n) * PZ]
        for comp in range(3):
            for n in range(7):
                r = (comp * 7 + n) * PZ
                face_row = n + 1
                if first_own <= face_row < first_own + 6:
                    y = own[face_row - first_own]
                    ue[r : r + PZ] = uu_ref[pl.ds(comp * UU_PLANE + y, PZ, stride=PLANE)]
                else:
                    m = (face_row - 1) if side == 0 else (face_row - 6)
                    q = (6 + 2 * comp + m) * PZ
                    ue[r : r + PZ] = face[q : q + PZ]

        def value_at(src, row):
            r = at(row)
            return advance(
                src[r : r + PZ],
                src[r + 1 : r + 1 + PZ],
                src[r - 1 : r - 1 + PZ],
                src[r + PZ : r + 2 * PZ],
                src[r - PZ : r],
                *[ue[(comp * 7 + row - 1) * PZ : (comp * 7 + row) * PZ] for comp in range(3)],
                lane,
            )

        def outside(row):
            return row < 3 if side == 0 else row >= 6

        for row in range(1, 8):
            value = value_at(se, row) * z_mask
            if outside(row):
                value = value * edge_ref[2 + side]
            fe[at(row) : at(row) + PZ] = value
        for row in range(2, 7):
            value = 0.75 * se[at(row) : at(row) + PZ] + 0.25 * value_at(fe, row)
            value = value * z_mask
            if outside(row):
                value = value * edge_ref[2 + side]
            ge[at(row) : at(row) + PZ] = value
        for row in range(3, 6):
            value = (1.0 / 3.0) * se[at(row) : at(row) + PZ] + (2.0 / 3.0) * value_at(ge, row)
            y = row - 3 if side == 0 else CY - 6 + row
            fe[at(row) : at(row) + PZ] = value
            for z in range(CZ):
                field_ref[z, y : y + 1, :] = fe[at(row) + 4 + z : at(row) + 5 + z]

    peak = jnp.zeros((8, CX), F32)
    for z in range(CZ):
        rows = field_ref[z, CY - TOP : CY, :]
        top[z * TOP : (z + 1) * TOP] = rows
        part = jnp.abs(field_ref[z, CY - TOP + 1 : CY, :])
        for k in range(0, TOP - 1, 8):
            peak = jnp.maximum(peak, part[k : k + 8])
        peak = jnp.maximum(peak, jnp.abs(rows[0:1]))
    most = jnp.max(peak)
    scales = pow_ref[...]
    step = jnp.sum((most > scales).astype(F32))
    index = lax.broadcasted_iota(jnp.int32, (1, CX), 1).astype(F32)
    scale = jnp.sum(jnp.where(index == step, scales, 0.0))
    shear_ref[0:SH_ROWS] = jnp.round(top[...] * (32000.0 / scale)).astype(I16)
    shear_ref[SH_ROWS : SH_ROWS + 16] = (jnp.zeros((16, CX), F32) + step).astype(I16)


def lights(shift_ref, frac_ref, color_ref, ext_ref, pow_ref, field_ref, shear_ref, out_ref, above, joined, turned):
    steps = shear_ref[SH_ROWS : SH_ROWS + 16].astype(F32)
    index = lax.broadcasted_iota(jnp.int32, (16, CX), 1).astype(F32)
    scale = jnp.max(jnp.where(index == steps, pow_ref[...], 0.0))
    above[0:SH_ROWS] = shear_ref[0:SH_ROWS].astype(F32) * (scale / 32000.0)
    for z in range(CZ):
        joined[z, 7:40, :] = above[z * TOP : (z + 1) * TOP]
        joined[z, 40:104, :] = field_ref[z]
    coeffs = [[color_ref[c, n] for n in range(4)] for c in range(3)]
    quad, const = ext_ref[0], ext_ref[1]
    HALF = 32
    for lo in range(0, CY, HALF):

        def one(z, state):
            trans, depth, red, green, blue = state
            start = 40 + lo - shift_ref[z]
            weight = frac_ref[z].astype(F32) * (1.0 / NFRAC)
            near = joined[z, pl.ds(start, HALF), :]
            far = joined[z, pl.ds(start - 1, HALF), :]
            g = (1.0 - weight) * near + weight * far
            optical = (quad * g * g + const) * (1.0 / 1024.0)
            fade = jnp.exp(-optical)
            share = trans * (1.0 - fade)
            sums = []
            for (a0, a1, a2, a3), total in zip(coeffs, (red, green, blue)):
                sums.append(total + share * (a0 + g * (a1 + g * (a2 + g * a3))))
            return (trans * fade, depth + optical, *sums)

        zero = jnp.zeros((HALF, CX), F32)
        _, depth, red, green, blue = lax.fori_loop(0, CZ, one, (zero + 1.0, zero, zero, zero, zero), unroll=2)
        for n, value in enumerate((red, green, blue, depth)):
            turned[n * CY + lo : n * CY + lo + HALF] = value
    for h in range(2):
        block = turned[h * 128 : (h + 1) * 128].T
        turned[h * 128 : (h + 1) * 128] = block
    for d in range(32):
        for h in range(2):
            out_ref[8 * d + 4 * h : 8 * d + 4 * h + 4] = turned[h * 128 + 4 * d : h * 128 + 4 * d + 4]


def finish(rank_ref, got_ref, image_ref, dep, order):
    for k in range(32):
        order[rank_ref[k]] = k
    got = got_ref[...].reshape(32, 8, 128)
    lane = lax.broadcasted_iota(jnp.int32, (32, 8, 128), 2)
    row = lax.broadcasted_iota(jnp.int32, (32, 8, 128), 1)
    depth = jnp.where(lane >= 64, got, pltpu.roll(got, 64, 2))
    depth = jnp.where(row >= 4, depth, pltpu.roll(depth, 4, 1))
    dep[...] = depth.reshape(256, 128)
    run = jnp.zeros((8, 128), F32)
    total = jnp.zeros((8, 128), F32)
    for r in range(32):
        base = pl.multiple_of(order[r] * 8, 8)
        total = total + jnp.exp(-run) * got_ref[pl.ds(base, 8)]
        run = run + dep[pl.ds(base, 8)]
    total = jnp.where((row[0] >= 4) & (lane[0] >= 64), 1.0 - jnp.exp(-run), total)
    for c in range(4):
        h, half = divmod(c, 2)
        image_ref[c] = total[4 * h : 4 * h + 4, 64 * half : 64 * half + 64]


def on_device(scalar, velocity, row_shift, frac_index, brick_rank, color_coeffs, extinction):
    gz, gy = lax.axis_index("gz"), lax.axis_index("gy")
    inside = jnp.stack([gz > 0, gz < lax.axis_size("gz") - 1, gy > 0, gy < lax.axis_size("gy") - 1]).astype(F32)
    pows = powers_of_two()

    z_face = shaped((12 * CY, CX), BF16)
    z_up, z_down = call(pack_z, (z_face, z_face), 0, 2)(scalar, velocity)
    z_below, z_above = shifted(z_up, "gz", 1), shifted(z_down, "gz", -1)

    y_face = shaped((12 * PZ, CX), BF16)
    ss, uu, y_up, y_down = call(
        assemble,
        (shaped((SS_ROWS, CX), F32), shaped((3 * UU_PLANE, CX), F32), y_face, y_face),
        0,
        4,
        [pltpu.VMEM((12 * PZ, CX), F32)],
    )(scalar, velocity, z_below, z_above)
    y_below, y_above = shifted(y_up, "gy", 1), shifted(y_down, "gy", -1)

    inner = call(
        stencil,
        shaped((CZ, CY, CX), F32),
        1,
        2,
        [pltpu.VMEM((SS_ROWS, CX), F32), pltpu.VMEM((SS_ROWS, CX), F32)],
        cost=(30000000, 6000000),
    )(inside, ss, uu)
    edge_rows = 9 * PZ + 16
    field, top = call(
        edges,
        (shaped((CZ, CY, CX), F32), shaped((SH_ROWS + 16, CX), I16)),
        1,
        6,
        [
            pltpu.VMEM((12 * PZ, CX), F32),
            pltpu.VMEM((edge_rows, CX), F32),
            pltpu.VMEM((21 * PZ, CX), F32),
            pltpu.VMEM((edge_rows, CX), F32),
            pltpu.VMEM((edge_rows, CX), F32),
            pltpu.VMEM((SH_ROWS, CX), F32),
        ],
    )(inside, pows, ss, uu, y_below, y_above, inner)
    above = shifted(top, "gy", 1)

    sent = call(
        lights,
        shaped((256, CX), F32),
        4,
        3,
        [
            pltpu.VMEM((SH_ROWS, CX), F32),
            pltpu.VMEM((CZ, 104, CX), F32),
            pltpu.VMEM((256, CX), F32),
        ],
    )(row_shift, frac_index, color_coeffs, extinction, pows, field, above)
    got = lax.all_to_all(sent.reshape(32, 8, CX), "gz", split_axis=0, concat_axis=0, tiled=True)

    image = call(
        finish,
        shaped((4, 4, CY), F32),
        1,
        1,
        [pltpu.VMEM((256, CX), F32), pltpu.SMEM((32,), jnp.int32)],
    )(brick_rank, got.reshape(256, CX))
    return field, jnp.transpose(image, (0, 2, 1))


def solution(mesh):
    placed = (P("gz", "gy", None), P(None, "gz", "gy", None), P("gz"), P("gz"), P(), P(), P())
    return jax.shard_map(
        on_device,
        mesh=mesh,
        in_specs=placed,
        out_specs=(P("gz", "gy", None), P(None, "gy", "gz")),
        check_vma=False,
    )
```

time: 104 us -> 66.9 us (0.64)
  other arithmetic: 29.2 us -> 0.08 us
  starting transfers between devices: 36.6 us -> 14.1 us
  blocking collectives: 0 us -> 17.5 us
  Pallas kernels: 0 us -> 14.3 us
  waiting for transfers between devices: 20.1 us -> 11.9 us
  local copies, waits for them, and re-layouts: 16 us -> 7.84 us
    all_to_all x0 -> x1, blocking collectives: none -> 17.5 us  [on_device(): lax.all_to_all(sent.reshape(32, 8, CX), 'gz', split_axis=0, concat_axis=0...]
    pallas_call x0 -> x6, Pallas kernels: none -> 14.3 us  [the longest x1 6.52 us: on_device(): call(stencil, shaped((CZ, CY, CX), F32), 1, 2, [pltpu.VMEM((SS_ROWS, CX),...]
    ppermute x9 -> x5, starting transfers between devices: 27.4 us -> 14.1 us  [shifted(): return lax.ppermute(value, axis, pairs)]
    add x3 -> x0, other arithmetic: 9.82 us -> none  [the longest x2 8.33 us: brick_light(): coeffs[0] + values * (coeffs[1] + values * (coeffs[2] + values * coeffs[3]))]
    all_to_all x1 -> x0, starting transfers between devices: 9.2 us -> none  [on_device(): lax.all_to_all(stacked, 'gz', split_axis=3, concat_axis=0, tiled=True)]
    gather x2 -> x0, local copies, waits for them, and re-layouts: 6.53 us -> none  [the longest x1 3.72 us: one_slice(): farther = lax.dynamic_slice_in_dim(slab, start - 1, height, 0)]
    all_to_all x1 -> x0, waiting for transfers between devices: 6 us -> none  [on_device(): lax.all_to_all(stacked, 'gz', split_axis=3, concat_axis=0, tiled=True)]
    another operation x1 -> x0, other arithmetic: 5.19 us -> none  [brick_light(): before = jnp.cumsum(optical, axis=0) - optical]
  transfers between devices with their start and end apart: 10 -> 5, of which waited for: 3 -> 3; matrix products, arithmetic and copies ran while one was open for 10% -> 0% of each run, Pallas kernels for 0% -> 10%
where the time goes in v1:
time: 66.9 us; the launch traced here: 66.5 us
  blocking collectives  17.5 us (26%)
  Pallas kernels  14.3 us (21%)
  starting transfers between devices  14.1 us (21%)
  waiting for transfers between devices  11.9 us (18%)
  local copies, waits for them, and re-layouts  7.84 us (12%)
  between operations  0.8 us (1%)
    all_to_all x1, blocking collectives, on_device(): lax.all_to_all(sent.reshape(32, 8, CX), 'gz', split_axis=0, concat_axis=0...  17.5 us
    ppermute x5, starting transfers between devices, shifted(): return lax.ppermute(value, axis, pairs)  14.1 us
    ppermute x5, waiting for transfers between devices, shifted(): return lax.ppermute(value, axis, pairs)  11.9 us
    unnamed x22, local copies, waits for them, and re-layouts  7.84 us
    pallas_call x1, Pallas kernels, on_device(): call(stencil, shaped((CZ, CY, CX), F32), 1, 2, [pltpu.VMEM((SS_ROWS, CX),...  6.52 us
    pallas_call x1, Pallas kernels, on_device(): call(edges, (shaped((CZ, CY, CX), F32), shaped((SH_ROWS + 16, CX), I16)),...  3.21 us
    pallas_call x1, Pallas kernels, on_device(): call(lights, shaped((256, CX), F32), 4, 3, [pltpu.VMEM((SH_ROWS, CX), F32...  2.56 us
    pallas_call x1, Pallas kernels, on_device(): call(finish, shaped((4, 4, CY), F32), 1, 1, [pltpu.VMEM((256, CX), F32),...  1.35 us
  transfers between devices with their start and end apart: 5, of which 3 were waited for; matrix products, arithmetic and copies ran while one was open for 0% of the time, Pallas kernels for 10%

profile of v1, /device:TPU:129, one launch (start us, length us, event | category | flops | bytes accessed | tf_op | source)
XLA Modules:
  0.0 66.5 jit_solution(5345000905337240211)
XLA Ops:
  0.6 0.0 copy-start.2
  0.6 1.4 %copy-done.2 = bf16[3,32,64,128]{3,2,1,0:T(8,128)(2,1)S(1)} copy-done((bf16[3,32,64,128]{3,2,1,0:T(8,128)(2,1)S(1)}, bf16[3,32,64,128]{3,2,1,0:T(8,128)(2,1)}, u32[]{:S(2)}) %copy-start.2) | copy-done | bytes 1572888
  2.0 1.2 %copy-done.3 = f32[32,64,128]{2,1,0:T(8,128)S(1)} copy-done((f32[32,64,128]{2,1,0:T(8,128)S(1)}, f32[32,64,128]{2,1,0:T(8,128)}, u32[]{:S(2)}) %copy-start.3) | copy-done | bytes 1048600
  3.3 3.7 %collective-permute-start = (bf16[768,128]{1,0:T(8,128)(2,1)S(1)}, bf16[768,128]{1,0:T(8,128)(2,1)S(1)}, u32[]{:S(2)}, u32[]{:S(2)}) collective-permute-start(bf16[768,128]{1,0:T(8,128)(2,1)S(1)} %get-tuple-element.10), channel_id=1, source_target_pairs={{0,1},{1,2},{2,3},{3,4},{4,5},{5,6},{6,7},{7,8},{8,9},{9,10},{10,1... | collective-permute-start | bytes 589832 | tf_op jit(solution)/shard_map/ppermute | solution.py:47
  7.0 1.9 %collective-permute-start.1 = (bf16[768,128]{1,0:T(8,128)(2,1)S(1)}, bf16[768,128]{1,0:T(8,128)(2,1)S(1)}, u32[]{:S(2)}, u32[]{:S(2)}) collective-permute-start(bf16[768,128]{1,0:T(8,128)(2,1)S(1)} %get-tuple-element.11), channel_id=1, source_target_pairs={{1,0},{2,1},{3,2},{4,3},{5,4},{6,5},{7,6},{8,7},{9,8},{10,9},{11,1... | collective-permute-start | bytes 589832 | tf_op jit(solution)/shard_map/ppermute | solution.py:47
  8.9 0.7 collective-permute-done.below_ref
  9.6 4.4 %collective-permute-done.1.above_ref = bf16[768,128]{1,0:T(8,128)(2,1)S(1)} collective-permute-done((bf16[768,128]{1,0:T(8,128)(2,1)S(1)}, bf16[768,128]{1,0:T(8,128)(2,1)S(1)}, u32[]{:S(2)}, u32[]{:S(2)}) %collective-permute-start.1) | collective-permute-done | bytes 196640 | tf_op jit(solution)/shard_map/ppermute | solution.py:47
  14.0 0.6 shard_map.96
  14.6 0.0 copy-start
  14.6 1.8 %copy-done = f32[7680,128]{1,0:T(8,128)} copy-done((f32[7680,128]{1,0:T(8,128)}, f32[7680,128]{1,0:T(8,128)S(1)}, u32[]{:S(2)}) %copy-start) | copy-done | bytes 3932184
  16.4 2.6 %collective-permute-start.2 = (bf16[480,128]{1,0:T(8,128)(2,1)S(1)}, bf16[480,128]{1,0:T(8,128)(2,1)S(1)}, u32[]{:S(2)}, u32[]{:S(2)}) collective-permute-start(bf16[480,128]{1,0:T(8,128)(2,1)S(1)} %get-tuple-element.14), channel_id=1, source_target_pairs={{0,32},{32,64},{64,96},{96,128},{128,160},{160,192},{192,224},{1,3... | collective-permute-start | bytes 368648 | tf_op jit(solution)/shard_map/ppermute | solution.py:47
  19.1 3.8 %collective-permute-start.3 = (bf16[480,128]{1,0:T(8,128)(2,1)S(1)}, bf16[480,128]{1,0:T(8,128)(2,1)S(1)}, u32[]{:S(2)}, u32[]{:S(2)}) collective-permute-start(bf16[480,128]{1,0:T(8,128)(2,1)S(1)} %get-tuple-element.15), channel_id=1, source_target_pairs={{32,0},{64,32},{96,64},{128,96},{160,128},{192,160},{224,192},{33,... | collective-permute-start | bytes 368648 | tf_op jit(solution)/shard_map/ppermute | solution.py:47
  22.9 0.1 add_convert_fusion.edge_ref
  23.0 2.1 %copy-done.1 = f32[7680,128]{1,0:T(8,128)S(1)} copy-done((f32[7680,128]{1,0:T(8,128)S(1)}, f32[7680,128]{1,0:T(8,128)}, u32[]{:S(2)}) %copy-start.1) | copy-done | bytes 3932184
  25.1 6.5 %shard_map.97.old_ref = f32[32,64,128]{2,1,0:T(8,128)S(1)} custom-call(f32[4]{0:T(128)S(1)} %add_convert_fusion.edge_ref, f32[2576,128]{1,0:T(8,128)S(1)} %get-tuple-element.12.ss_ref, f32[7680,128]{1,0:T(8,128)S(1)} %copy-done.1), custom_call_target="tpu_custom_call" | custom-call | flops 30000000 | bytes 6000000 | tf_op jit(solution)/shard_map/pallas_call | solution.py:333
  31.6 0.0 copy-start.5
  31.7 0.0 copy-start.7
  31.7 0.0 copy-start.8
  31.7 0.0 copy-start.9
  31.7 0.0 collective-permute-done.2.below_ref
  31.7 0.0 collective-permute-done.3.above_ref
  31.7 0.0 copy-done.6
  31.7 3.2 %shard_map.98 = (f32[32,64,128]{2,1,0:T(8,128)}, s16[1072,128]{1,0:T(8,128)(2,1)S(1)}) custom-call(f32[4]{0:T(128)S(1)} %add_convert_fusion.edge_ref, f32[1,128]{1,0:T(1,128)S(1)} %copy-done.6, f32[2576,128]{1,0:T(8,128)S(1)} %get-tuple-element.12.ss_ref, f32[7680,128]{1,0:T(8,128)S(1)} %copy-done.1, bf16[480,128]{1,0:T(8,128)(2,1)S(1)} %collective-permute-done.2.below_ref, ...), custom_call_target="tpu_custom_call" | custom-call | flops 1000000 | bytes 1000000 | tf_op jit(solution)/shard_map/pallas_call | solution.py:342
  34.9 2.0 %collective-permute-start.4 = (s16[1072,128]{1,0:T(8,128)(2,1)S(1)}, s16[1072,128]{1,0:T(8,128)(2,1)S(1)}, u32[]{:S(2)}, u32[]{:S(2)}) collective-permute-start(s16[1072,128]{1,0:T(8,128)(2,1)S(1)} %get-tuple-element.17), channel_id=1, source_target_pairs={{0,32},{32,64},{64,96},{96,128},{128,160},{160,192},{192,224},{1,3... | collective-permute-start | bytes 823304 | tf_op jit(solution)/shard_map/ppermute | solution.py:47
  37.0 6.8 %collective-permute-done.4.shear_ref = s16[1072,128]{1,0:T(8,128)(2,1)S(1)} collective-permute-done((s16[1072,128]{1,0:T(8,128)(2,1)S(1)}, s16[1072,128]{1,0:T(8,128)(2,1)S(1)}, u32[]{:S(2)}, u32[]{:S(2)}) %collective-permute-start.4) | collective-permute-done | bytes 274464 | tf_op jit(solution)/shard_map/ppermute | solution.py:47
  43.8 0.0 copy-done.7
  43.9 0.0 copy-start.4
  43.9 1.2 %copy-done.4 = f32[32,64,128]{2,1,0:T(8,128)S(1)} copy-done((f32[32,64,128]{2,1,0:T(8,128)S(1)}, f32[32,64,128]{2,1,0:T(8,128)}, u32[]{:S(2)}) %copy-start.4) | copy-done | bytes 1048600
  45.1 2.6 %shard_map.99 = f32[256,128]{1,0:T(8,128)S(1)} custom-call(s32[32]{0:T(128)S(1)} %copy-done.7, s32[32]{0:T(128)S(1)} %copy-done.8, f32[3,4]{1,0:T(4,128)S(1)} %copy-done.5, f32[2]{0:T(128)S(1)} %copy-done.9, f32[1,128]{1,0:T(1,128)S(1)} %copy-done.6, f32[32,64,128]{2,1,0:T(8,128)S(1)} %copy-done.4, s16[1072,128]{1,0:T(8,128)(2,1)S(1)} %collective-permute-done.4.shear_ref), custom_call_target="tpu_custom_call" | custom-call | flops 1000000 | bytes 1000000 | tf_op jit(solution)/shard_map/pallas_call | solution.py:358
  47.7 17.5 %all_to_all.5 = f32[32,8,128]{2,1,0:T(8,128)S(1)} all-to-all(f32[32,8,128]{2,1,0:T(8,128)S(1)} %bitcast.7), channel_id=1, replica_groups=mesh['gy'=8,'gz'=32] {'gz'}, dimensions={0} | all-to-all | bytes 262144 | tf_op jit(solution)/shard_map/all_to_all | solution.py:369
  65.2 0.0 copy-done.10
  65.2 1.4 %shard_map.100 = f32[4,4,64]{2,1,0:T(4,128)} custom-call(s32[32]{0:T(128)S(1)} %copy-done.10, f32[256,128]{1,0:T(8,128)S(1)} %bitcast.8), custom_call_target="tpu_custom_call" | custom-call | flops 1000000 | bytes 1000000 | tf_op jit(solution)/shard_map/pallas_call | solution.py:371
  (8 shorter events, 0.0 us)
Async XLA Ops:
  0.6 1.4 %copy-start.2 = (bf16[3,32,64,128]{3,2,1,0:T(8,128)(2,1)S(1)}, bf16[3,32,64,128]{3,2,1,0:T(8,128)(2,1)}, u32[]{:S(2)}) copy-start(bf16[3,32,64,128]{3,2,1,0:T(8,128)(2,1)} %u_ref.3) | copy-start | bytes 4718596
  2.0 1.2 %copy-start.3 = (f32[32,64,128]{2,1,0:T(8,128)S(1)}, f32[32,64,128]{2,1,0:T(8,128)}, u32[]{:S(2)}) copy-start(f32[32,64,128]{2,1,0:T(8,128)} %s_ref.3) | copy-start | bytes 3145732
  3.3 6.3 %collective-permute-start = (bf16[768,128]{1,0:T(8,128)(2,1)S(1)}, bf16[768,128]{1,0:T(8,128)(2,1)S(1)}, u32[]{:S(2)}, u32[]{:S(2)}) collective-permute-start(bf16[768,128]{1,0:T(8,128)(2,1)S(1)} %get-tuple-element.10), channel_id=1, source_target_pairs={{0,1},{1,2},{2,3},{3,4},{4,5},{5,6},{6,7},{7,8},{8,9},{9,10},{10,1... | collective-permute-start | bytes 589832 | tf_op jit(solution)/shard_map/ppermute | solution.py:47
  7.0 7.0 %collective-permute-start.1 = (bf16[768,128]{1,0:T(8,128)(2,1)S(1)}, bf16[768,128]{1,0:T(8,128)(2,1)S(1)}, u32[]{:S(2)}, u32[]{:S(2)}) collective-permute-start(bf16[768,128]{1,0:T(8,128)(2,1)S(1)} %get-tuple-element.11), channel_id=1, source_target_pairs={{1,0},{2,1},{3,2},{4,3},{5,4},{6,5},{7,6},{8,7},{9,8},{10,9},{11,1... | collective-permute-start | bytes 589832 | tf_op jit(solution)/shard_map/ppermute | solution.py:47
  14.6 1.9 %copy-start = (f32[7680,128]{1,0:T(8,128)}, f32[7680,128]{1,0:T(8,128)S(1)}, u32[]{:S(2)}) copy-start(f32[7680,128]{1,0:T(8,128)S(1)} %get-tuple-element.13.uu_ref) | copy-start | bytes 11796484
  16.4 15.3 %collective-permute-start.2 = (bf16[480,128]{1,0:T(8,128)(2,1)S(1)}, bf16[480,128]{1,0:T(8,128)(2,1)S(1)}, u32[]{:S(2)}, u32[]{:S(2)}) collective-permute-start(bf16[480,128]{1,0:T(8,128)(2,1)S(1)} %get-tuple-element.14), channel_id=1, source_target_pairs={{0,32},{32,64},{64,96},{96,128},{128,160},{160,192},{192,224},{1,3... | collective-permute-start | bytes 368648 | tf_op jit(solution)/shard_map/ppermute | solution.py:47
  19.1 12.7 %collective-permute-start.3 = (bf16[480,128]{1,0:T(8,128)(2,1)S(1)}, bf16[480,128]{1,0:T(8,128)(2,1)S(1)}, u32[]{:S(2)}, u32[]{:S(2)}) collective-permute-start(bf16[480,128]{1,0:T(8,128)(2,1)S(1)} %get-tuple-element.15), channel_id=1, source_target_pairs={{32,0},{64,32},{96,64},{128,96},{160,128},{192,160},{224,192},{33,... | collective-permute-start | bytes 368648 | tf_op jit(solution)/shard_map/ppermute | solution.py:47
  23.0 2.1 %copy-start.1 = (f32[7680,128]{1,0:T(8,128)S(1)}, f32[7680,128]{1,0:T(8,128)}, u32[]{:S(2)}) copy-start(f32[7680,128]{1,0:T(8,128)} %copy-done) | copy-start | bytes 11796484
  25.1 6.6 %copy-start.6 = (f32[1,128]{1,0:T(1,128)S(1)}, f32[1,128]{1,0:T(1,128)}, u32[]{:S(2)}) copy-start(f32[1,128]{1,0:T(1,128)} %constant.17.clone.pow_ref) | copy-start | bytes 1540
  31.6 12.2 %copy-start.5 = (f32[3,4]{1,0:T(4,128)S(1)}, f32[3,4]{1,0:T(4,128)}, u32[]{:S(2)}) copy-start(f32[3,4]{1,0:T(4,128)} %color_ref.1) | copy-start | bytes 148
  31.7 12.2 %copy-start.7 = (s32[32]{0:T(128)S(1)}, s32[32]{0:T(128)}, u32[]{:S(2)}) copy-start(s32[32]{0:T(128)} %shift_ref.1) | copy-start | bytes 388
  31.7 12.2 %copy-start.8 = (s32[32]{0:T(128)S(1)}, s32[32]{0:T(128)}, u32[]{:S(2)}) copy-start(s32[32]{0:T(128)} %frac_ref.1) | copy-start | bytes 388
  31.7 12.2 %copy-start.9 = (f32[2]{0:T(128)S(1)}, f32[2]{0:T(128)}, u32[]{:S(2)}) copy-start(f32[2]{0:T(128)} %ext_ref.1) | copy-start | bytes 28
  34.9 30.2 %copy-start.10 = (s32[32]{0:T(128)S(1)}, s32[32]{0:T(128)}, u32[]{:S(2)}) copy-start(s32[32]{0:T(128)} %rank_ref.1) | copy-start | bytes 388
  34.9 8.9 %collective-permute-start.4 = (s16[1072,128]{1,0:T(8,128)(2,1)S(1)}, s16[1072,128]{1,0:T(8,128)(2,1)S(1)}, u32[]{:S(2)}, u32[]{:S(2)}) collective-permute-start(s16[1072,128]{1,0:T(8,128)(2,1)S(1)} %get-tuple-element.17), channel_id=1, source_target_pairs={{0,32},{32,64},{64,96},{96,128},{128,160},{160,192},{192,224},{1,3... | collective-permute-start | bytes 823304 | tf_op jit(solution)/shard_map/ppermute | solution.py:47
  43.9 1.2 %copy-start.4 = (f32[32,64,128]{2,1,0:T(8,128)S(1)}, f32[32,64,128]{2,1,0:T(8,128)}, u32[]{:S(2)}) copy-start(f32[32,64,128]{2,1,0:T(8,128)} %get-tuple-element.8.field_ref) | copy-start | bytes 3145732

commit v2 on v0

v2 whole, which is shorter than its diff:
```python
import jax
import jax.numpy as jnp
import numpy as np
from jax import lax
from jax.experimental import pallas as pl
from jax.experimental.pallas import tpu as pltpu
from jax.sharding import PartitionSpec as P


NFRAC = 8
SHIFT_MAX = 32
CZ, CY, CX = 32, 64, 128
PZ = 40
PLANE = CY
SS_ROWS = PZ * PLANE + 16
CELLS = CZ * CY
UE_ROWS = 6 * PZ * 8
J_ROWS = 80
UP, DOWN = 6, 3
UP_ROWS, DOWN_ROWS = 1088, 480
TOP = SHIFT_MAX + 1 - 3
SH_ROWS = CZ * TOP
F32, BF16, I16 = jnp.float32, jnp.bfloat16, jnp.int16
VM = pl.BlockSpec(memory_space=pltpu.VMEM)
SM = pl.BlockSpec(memory_space=pltpu.SMEM)
HB = pl.BlockSpec(memory_space=pltpu.HBM)


def call(kernel, outs, ins, scratch=(), aliases=None, out_specs=None, cycles=1000, vmem=16777216):
    return pl.pallas_call(
        kernel,
        out_shape=outs,
        in_specs=list(ins),
        out_specs=out_specs or jax.tree.map(lambda _: VM, outs),
        scratch_shapes=list(scratch),
        input_output_aliases=aliases or {},
        compiler_params=pltpu.CompilerParams(vmem_limit_bytes=vmem),
        cost_estimate=pl.CostEstimate(flops=4096 * cycles, bytes_accessed=1024 * cycles, transcendentals=0),
    )


def shaped(shape, dtype):
    return jax.ShapeDtypeStruct(shape, dtype)


def shifted(value, axis, by):
    count = lax.axis_size(axis)
    pairs = [(i, i + by) for i in range(count) if 0 <= i + by < count]
    return lax.ppermute(value, axis, pairs)


def split(value):
    high = value.astype(BF16)
    return high, (value - high.astype(F32)).astype(BF16)


def powers_of_two():
    return jnp.asarray(np.repeat((2.0 ** (np.arange(128) - 110.0)).astype(np.float32)[:, None], CX, 1))


def pack_z(s_ref, u_ref, up_ref, down_ref, s_buf, u_buf, sem):
    copies = []
    for side, (s_lo, u_lo) in enumerate(((CZ - 3, CZ - 2), (0, 0))):
        copies.append(pltpu.make_async_copy(s_ref.at[pl.ds(s_lo * CY, 3 * CY)], s_buf.at[side], sem.at[2 * side]))
        copies.append(pltpu.make_async_copy(u_ref.at[:, pl.ds(u_lo, 2)], u_buf.at[side], sem.at[2 * side + 1]))
    for copy in copies:
        copy.start()
    for side, out in enumerate((up_ref, down_ref)):
        copies[2 * side].wait()
        high, low = split(s_buf[side])
        out[0 : 3 * CY] = high
        out[3 * CY : 6 * CY] = low
        copies[2 * side + 1].wait()
        for comp in range(3):
            out[(6 + 2 * comp) * CY : (8 + 2 * comp) * CY] = u_buf[side, comp].reshape(2 * CY, CX)


def flat(z):
    return 8 + PLANE * (z + 4)


def aligned(x):
    return x if isinstance(x, int) else pl.multiple_of(x, 8)


def advance(c, zn, zp, yn, yp, uz, uy, ux, lane):
    xn = jnp.where(lane == CX - 1, 0.0, pltpu.roll(c, CX - 1, 1))
    xp = jnp.where(lane == 0, 0.0, pltpu.roll(c, 1, 1))
    total = (zn + zp) + (yn + yp) + (xn + xp)
    flow = uz * (zn - zp) + uy * (yn - yp) + ux * (xn - xp)
    return 0.94 * c + (0.01 * total - 0.1 * flow)


FULL = ((0, 16), (16, 16), (32, 16), (48, 16))
UPPER = ((24, 8), (32, 16), (48, 16))
UPPER_2, LOWER_2 = ((16, 16), (32, 16), (48, 16)), ((0, 16),)
EARLY = 14
LOWER = ((0, 16), (16, 8))


def one_plane(src, z, u_of, put, chunks=FULL):
    base = aligned(flat(z))
    near = src.at[pl.ds(aligned(base - 8), CY + 16)]
    after = src.at[pl.ds(aligned(base + PLANE), CY)]
    before = src.at[pl.ds(aligned(base - PLANE), CY)]
    for k, n in chunks:
        lane = lax.broadcasted_iota(jnp.int32, (n, CX), 1)
        value = advance(
            near[8 + k : 8 + k + n],
            after[k : k + n],
            before[k : k + n],
            near[9 + k : 9 + k + n],
            near[7 + k : 7 + k + n],
            *[u_of(comp, k, n).astype(F32) for comp in range(3)],
            lane,
        )
        put(aligned(base + k), k, n, value)


def run_planes(lo, hi, step, body):
    trips = (hi - lo) // step

    def group(i, _):
        for n in range(step):
            body(lo + i * step + n)
        return 0

    lax.fori_loop(0, trips, group, 0)
    for z in range(lo + trips * step, hi):
        body(z)


def own_velocity(u_ref, z):
    return lambda comp, k, n: u_ref[comp, z, k : k + n, :]


def any_velocity(u_ref, below_ref, above_ref, z):
    if 0 <= z < CZ:
        return own_velocity(u_ref, z)
    ref, plane = (below_ref, z + 2) if z < 0 else (above_ref, z - CZ)

    def of(comp, k, n):
        base = (6 + 2 * comp + plane) * CY + k
        return ref[base : base + n]

    return of


def put_first(f1):
    def put(at, k, n, value):
        f1[pl.ds(at, n)] = value

    return put


def put_second(f2, ss_ref):
    def put(at, k, n, value):
        f2[pl.ds(at, n)] = 0.75 * ss_ref[pl.ds(at, n)] + 0.25 * value

    return put


def put_field(field_ref, ss_ref):
    def put(at, k, n, value):
        to = aligned(at - flat(0))
        field_ref[pl.ds(to, n)] = (1.0 / 3.0) * ss_ref[pl.ds(at, n)] + (2.0 / 3.0) * value

    return put


GROUP = 8


def inner(s_ref, u_ref, ss_ref, uv_ref, ue_ref, f1, f2, sem):
    copies = []
    for c in range(CZ // GROUP):
        rows = GROUP * CY
        copies.append(
            (
                pltpu.make_async_copy(s_ref.at[pl.ds(c * rows, rows)], ss_ref.at[pl.ds(flat(0) + c * rows, rows)], sem.at[2 * c]),
                pltpu.make_async_copy(u_ref.at[:, pl.ds(c * GROUP, GROUP)], uv_ref.at[:, pl.ds(c * GROUP, GROUP)], sem.at[2 * c + 1]),
            )
        )
    for pair in copies:
        for copy in pair:
            copy.start()

    def take(z):
        for comp in range(3):
            for side, k in ((0, 0), (1, CY - 16)):
                rows = uv_ref[comp, z, k : k + 16, :].astype(F32)
                to = ((2 * comp + side) * PZ + 4 + z) * 8
                ue_ref[pl.ds(aligned(to), 8)] = rows[8 * side : 8 * side + 8]

    for c, pair in enumerate(copies):
        for copy in pair:
            copy.wait()
        lo, hi = max(1, GROUP * c - 1), GROUP * (c + 1) - 1
        run_planes(lo, hi, 4, lambda z: one_plane(ss_ref, z, own_velocity(uv_ref, z), put_first(f1)))
        run_planes(GROUP * c, GROUP * (c + 1), 4, take)
    run_planes(2, EARLY, 4, lambda z: one_plane(f1, z, own_velocity(uv_ref, z), put_second(f2, ss_ref), UPPER_2))


def assemble(below_ref, above_ref, ss_in, ue_in, ss_ref, ue_ref, up_ref, down_ref, face):
    for halo, z in ((below_ref, -3), (above_ref, CZ)):
        ss_ref[flat(z) : flat(z) + 3 * CY] = halo[0 : 3 * CY].astype(F32) + halo[3 * CY : 6 * CY].astype(F32)
    for comp in range(3):
        for halo, z in ((below_ref, -2), (above_ref, CZ)):
            for n in range(2):
                base = (6 + 2 * comp + n) * CY
                for side, k in ((0, 0), (1, CY - 16)):
                    rows = halo[base + k : base + k + 16].astype(F32)
                    to = ((2 * comp + side) * PZ + 4 + z + n) * 8
                    ue_ref[to : to + 8] = rows[8 * side : 8 * side + 8]
    for side, out, count, s_lo in ((1, up_ref, UP, CY - UP), (0, down_ref, DOWN, 0)):
        for row in range(count):
            value = ss_ref[pl.ds(8 + s_lo + row, PZ, stride=PLANE)]
            high = value.astype(BF16).astype(F32)
            face[row * PZ : (row + 1) * PZ] = high
            face[(count + row) * PZ : (count + row + 1) * PZ] = value - high
        for comp in range(3):
            for row in range(count - 1):
                at = 2 * count + (count - 1) * comp + row
                start = (2 * comp + side) * PZ * 8 + (8 - (count - 1) if side else 0) + row
                face[at * PZ : (at + 1) * PZ] = ue_ref[pl.ds(start, PZ, stride=8)]
        out[...] = face[0 : out.shape[0]].astype(BF16)


def inside(axis, side):
    place = lax.axis_index(axis)
    return jnp.where(place == (lax.axis_size(axis) - 1) * side, 0.0, 1.0)


def middle(pow_ref, u_ref, below_ref, above_ref, ss_ref, f1_in, f2_in, f1, f2, field_ref, shear_ref, top):
    def velocity(z):
        return any_velocity(u_ref, below_ref, above_ref, z)

    def mask(dst, width):
        for z, side in ((-width, 0), (CZ, 1)):
            rows = slice(flat(z), flat(z) + width * CY)
            dst[rows] = dst[rows] * inside("gz", side)

    for z in (-2, -1, 0, CZ - 1, CZ, CZ + 1):
        one_plane(ss_ref, z, velocity(z), put_first(f1))
    mask(f1, 2)
    for z in (-1, 0, 1, CZ):
        one_plane(f1, z, velocity(z), put_second(f2, ss_ref), UPPER_2)
    run_planes(EARLY, CZ, 3, lambda z: one_plane(f1, z, own_velocity(u_ref, z), put_second(f2, ss_ref), UPPER_2))
    mask(f2, 1)
    run_planes(0, CZ, 4, lambda z: one_plane(f2, z, own_velocity(u_ref, z), put_field(field_ref, ss_ref), UPPER))
    for z in range(CZ):
        top[z * TOP : (z + 1) * TOP] = field_ref[z * CY + CY - TOP - 3 : (z + 1) * CY - 3]
    peak = jnp.max(jnp.abs(top[...]), axis=0, keepdims=True)
    enough = pow_ref[...] >= peak
    scale = jnp.min(jnp.where(enough, pow_ref[...], 2.0**17), axis=0, keepdims=True)
    step = jnp.sum(jnp.where(enough, 0.0, 1.0), axis=0, keepdims=True)
    shear_ref[0:SH_ROWS] = jnp.round(top[...] * (32000.0 / scale)).astype(I16)
    shear_ref[SH_ROWS : SH_ROWS + 16] = jnp.broadcast_to(step, (16, CX)).astype(I16)


def fix_rows(side, ss_ref, ue_ref, halo, field_ref, joined, face, se, fe, ge):
    count = (UP, DOWN)[side]
    first_own, first_halo, y_own, total = ((UP, 0, 0, UP + 6), (0, 6, CY - 6, 6 + DOWN))[side]
    lane = lax.broadcasted_iota(jnp.int32, (PZ, CX), 1)
    spot = lax.broadcasted_iota(jnp.int32, (PZ, CX), 0)
    z_mask = jnp.where(spot < 4, inside("gz", 0), jnp.where(spot >= 4 + CZ, inside("gz", 1), 1.0))
    y_mask = z_mask * inside("gy", side)
    face[0 : halo.shape[0]] = halo[...].astype(F32)

    def at(row):
        return 8 + row * PZ

    def beyond(row):
        return not first_own <= row < first_own + 6

    for n in range(6):
        r = at(first_own + n)
        se[r : r + PZ] = ss_ref[pl.ds(8 + y_own + n, PZ, stride=PLANE)]
    for n in range(count):
        r = at(first_halo + n)
        se[r : r + PZ] = face[n * PZ : (n + 1) * PZ] + face[(count + n) * PZ : (count + n + 1) * PZ]

    def velocity(comp, row):
        if not beyond(row):
            start = (2 * comp + side) * PZ * 8 + (y_own + row - first_own) % 8
            return ue_ref[pl.ds(start, PZ, stride=8)]
        q = (2 * count + (count - 1) * comp + (row - 1 if side == 0 else row - 6)) * PZ
        return face[q : q + PZ]

    def value_at(src, row):
        r = at(row)
        return advance(
            src[r : r + PZ],
            src[r + 1 : r + 1 + PZ],
            src[r - 1 : r - 1 + PZ],
            src[r + PZ : r + 2 * PZ],
            src[r - PZ : r],
            *[velocity(comp, row) for comp in range(3)],
            lane,
        )

    for row in range(1, total - 1):
        fe[at(row) : at(row) + PZ] = value_at(se, row) * (y_mask if beyond(row) else z_mask)
    for row in range(2, total - 2):
        r = at(row)
        ge[r : r + PZ] = (0.75 * se[r : r + PZ] + 0.25 * value_at(fe, row)) * (y_mask if beyond(row) else z_mask)
    for row in range(3, total - 3):
        r = at(row)
        value = ((1.0 / 3.0) * se[r : r + PZ] + (2.0 / 3.0) * value_at(ge, row))[4 : 4 + CZ]
        if beyond(row):
            joined[pl.ds(40 + row - first_own, CZ, stride=J_ROWS)] = value * inside("gy", side)
        else:
            field_ref[pl.ds(y_own + row - first_own, CZ, stride=CY)] = value


FACE_ROWS = 12 * PZ + 16


LOG2E = 1.4426950408889634


def march(shift_ref, frac_ref, ext_ref, src, start, n, mom_ref, lo):
    quad = ext_ref[0] * (-LOG2E / 1024.0)
    const = ext_ref[1] * (-LOG2E / 1024.0)

    def one(z, state):
        trans, depth, m1, m2, m3 = state
        at = start(z) - shift_ref[z]
        weight = frac_ref[z].astype(F32) * (1.0 / NFRAC)
        near = src[pl.ds(at, n), :]
        far = src[pl.ds(at - 1, n), :]
        g = (1.0 - weight) * near + weight * far
        g2 = g * g
        power = quad * g2 + const
        left = trans * jnp.exp2(power)
        share = trans - left
        s1 = share * g
        s2 = share * g2
        return left, depth + power, m1 + s1, m2 + s2, m3 + s2 * g

    zero = jnp.zeros((n, CX), F32)
    trans, depth, m1, m2, m3 = lax.fori_loop(0, CZ, one, (zero + 1.0, zero, zero, zero, zero), unroll=4)
    for i, value in enumerate((1.0 - trans, m1, m2, m3, depth * (-1.0 / LOG2E))):
        mom_ref[i * CY + lo : i * CY + lo + n] = value


def lower(u_ref, below_ref, above_ref, ss_ref, f1, f2_in, field_in, f2, field_ref):
    for z in (-1, CZ):
        one_plane(f1, z, any_velocity(u_ref, below_ref, above_ref, z), put_second(f2, ss_ref), LOWER_2)
        rows = slice(flat(z), flat(z) + 16)
        f2[rows] = f2[rows] * inside("gz", int(z == CZ))
    run_planes(0, CZ, 4, lambda z: one_plane(f1, z, own_velocity(u_ref, z), put_second(f2, ss_ref), LOWER_2))
    run_planes(0, CZ, 4, lambda z: one_plane(f2, z, own_velocity(u_ref, z), put_field(field_ref, ss_ref), LOWER))


def borders(shift_ref, frac_ref, ext_ref, ss_ref, ue_ref, below_ref, above_ref, field_in,
            field_ref, out_ref, joined, mom_ref, face, se, fe, ge, sem):
    fix_rows(0, ss_ref, ue_ref, below_ref, field_ref, joined, face, se, fe, ge)
    fix_rows(1, ss_ref, ue_ref, above_ref, field_ref, joined, face, se, fe, ge)
    copy = pltpu.make_async_copy(field_ref, out_ref, sem)
    copy.start()
    march(shift_ref, frac_ref, ext_ref, field_ref, lambda z: z * CY + 40, 24, mom_ref, 40)
    for z in range(CZ):
        joined[z * J_ROWS + 40 : z * J_ROWS + 80] = field_ref[z * CY : z * CY + 40]
    copy.wait()


def lights(shift_ref, frac_ref, color_ref, ext_ref, pow_ref, shear_ref, joined_in, mom_in, out_ref, joined, mom_ref, above, turned):
    step = shear_ref[SH_ROWS : SH_ROWS + 16].astype(F32)[0:1]
    index = lax.broadcasted_iota(jnp.int32, (128, CX), 0).astype(F32)
    scale = jnp.sum(jnp.where(index == step, pow_ref[...], 0.0), axis=0, keepdims=True)
    above[...] = shear_ref[0:SH_ROWS].astype(F32) * (scale * (1.0 / 32000.0))
    for z in range(CZ):
        joined[z * J_ROWS + 7 : z * J_ROWS + 37] = above[z * TOP : (z + 1) * TOP]
    march(shift_ref, frac_ref, ext_ref, joined, lambda z: z * J_ROWS + 40, 40, mom_ref, 0)
    moments = [mom_ref[i * CY : (i + 1) * CY] for i in range(5)]
    for c in range(3):
        turned[c * CY : (c + 1) * CY] = (color_ref[c, 0] * moments[0] + color_ref[c, 1] * moments[1]) + (
            color_ref[c, 2] * moments[2] + color_ref[c, 3] * moments[3]
        )
    turned[3 * CY : 4 * CY] = moments[4]
    for h in range(2):
        turned[h * 128 : (h + 1) * 128] = turned[h * 128 : (h + 1) * 128].T
    for d in range(32):
        for h in range(2):
            out_ref[8 * d + 4 * h : 8 * d + 4 * h + 4] = turned[h * 128 + 4 * d : h * 128 + 4 * d + 4]


def finish(rank_ref, got_ref, image_ref, dep, order):
    for k in range(32):
        order[rank_ref[k]] = k
    got = got_ref[...].reshape(32, 8, 128)
    lane = lax.broadcasted_iota(jnp.int32, (32, 8, 128), 2)
    row = lax.broadcasted_iota(jnp.int32, (32, 8, 128), 1)
    depth = jnp.where(lane >= 64, got, pltpu.roll(got, 64, 2))
    depth = jnp.where(row >= 4, depth, pltpu.roll(depth, 4, 1))
    dep[...] = depth.reshape(256, 128)
    run = jnp.zeros((8, 128), F32)
    total = jnp.zeros((8, 128), F32)
    for r in range(32):
        base = pl.multiple_of(order[r] * 8, 8)
        total = total + jnp.exp(-run) * got_ref[pl.ds(base, 8)]
        run = run + dep[pl.ds(base, 8)]
    total = jnp.where((row[0] >= 4) & (lane[0] >= 64), 1.0 - jnp.exp(-run), total)
    for c in range(4):
        h, half = divmod(c, 2)
        image_ref[c] = total[4 * h : 4 * h + 4, 64 * half : 64 * half + 64]


def on_device(scalar, velocity, row_shift, frac_index, brick_rank, color_coeffs, extinction):
    powers = powers_of_two()
    hbm_scalar = pltpu.with_memory_space_constraint(scalar.reshape(CELLS, CX), pltpu.HBM)
    hbm_velocity = pltpu.with_memory_space_constraint(velocity, pltpu.HBM)

    z_face = shaped((12 * CY, CX), BF16)
    z_up, z_down = call(
        pack_z,
        (z_face, z_face),
        [HB, HB],
        [pltpu.VMEM((2, 3 * CY, CX), F32), pltpu.VMEM((2, 3, 2, CY, CX), BF16), pltpu.SemaphoreType.DMA((4,))],
    )(hbm_scalar, hbm_velocity)
    z_below, z_above = shifted(z_up, "gz", 1), shifted(z_down, "gz", -1)

    padded, slab = shaped((SS_ROWS, CX), F32), shaped((CELLS, CX), F32)
    rows, speed = shaped((UE_ROWS, CX), F32), shaped((3, CZ, CY, CX), BF16)
    ss, uv, ue, f1, f2 = call(
        inner, (padded, speed, rows, padded, padded), [HB, HB], [pltpu.SemaphoreType.DMA((8,))], cycles=3000
    )(hbm_scalar, hbm_velocity)

    ss, ue, y_up, y_down = call(
        assemble,
        (padded, rows, shaped((UP_ROWS, CX), BF16), shaped((DOWN_ROWS, CX), BF16)),
        [VM] * 4,
        [pltpu.VMEM((UP_ROWS, CX), F32)],
        {2: 0, 3: 1},
    )(z_below, z_above, ss, ue)
    y_below = shifted(y_up, "gy", 1)
    y_above = shifted(y_down, "gy", -1)

    f1, f2, field, top = call(
        middle,
        (padded, padded, slab, shaped((SH_ROWS + 16, CX), I16)),
        [VM] * 7,
        [pltpu.VMEM((SH_ROWS, CX), F32)],
        {5: 0, 6: 1},
        cycles=2500,
    )(powers, uv, z_below, z_above, ss, f1, f2)
    above = shifted(top, "gy", 1)

    joined_shape, moments_shape = shaped((CZ * J_ROWS, CX), F32), shaped((5 * CY, CX), F32)
    _, field = call(lower, (padded, slab), [VM] * 7, (), {5: 0, 6: 1}, cycles=1000)(
        uv, z_below, z_above, ss, f1, f2, field
    )
    _, field_out, joined, moments = call(
        borders,
        (slab, slab, joined_shape, moments_shape),
        [SM] * 3 + [VM] * 5,
        [pltpu.VMEM((UP_ROWS, CX), F32)] + [pltpu.VMEM((FACE_ROWS, CX), F32)] * 3 + [pltpu.SemaphoreType.DMA],
        {7: 0},
        (VM, HB, VM, VM),
        cycles=2500,
    )(row_shift, frac_index, extinction, ss, ue, y_below, y_above, field)
    sent, _, _ = call(
        lights,
        (shaped((256, CX), F32), joined_shape, moments_shape),
        [SM] * 4 + [VM] * 4,
        [pltpu.VMEM((SH_ROWS, CX), F32), pltpu.VMEM((256, CX), F32)],
        {6: 1, 7: 2},
    )(row_shift, frac_index, color_coeffs, extinction, powers, above, joined, moments)
    got = lax.all_to_all(sent.reshape(32, 8, CX), "gz", split_axis=0, concat_axis=0, tiled=True)

    image = call(
        finish,
        shaped((4, 4, CY), F32),
        [SM, VM],
        [pltpu.VMEM((256, CX), F32), pltpu.SMEM((32,), jnp.int32)],
    )(brick_rank, got.reshape(256, CX))
    return field_out.reshape(CZ, CY, CX), jnp.transpose(image, (0, 2, 1))


def solution(mesh):
    placed = (P("gz", "gy", None), P(None, "gz", "gy", None), P("gz"), P("gz"), P(), P(), P())
    return jax.shard_map(
        on_device,
        mesh=mesh,
        in_specs=placed,
        out_specs=(P("gz", "gy", None), P(None, "gy", "gz")),
        check_vma=False,
    )
```

time: 104 us -> 51 us (0.49)
  the two profiles are of different devices: /device:TPU:129 before, /device:TPU:97 now
where the time goes in v2:
time: 51 us; the launch traced here: 50.7 us
  blocking collectives  16.2 us (32%)
  starting transfers between devices  15.6 us (31%)
  Pallas kernels  13.4 us (26%)
  waiting for transfers between devices  4.63 us (9%)
  between operations  0.8 us (2%)
    all_to_all x1, blocking collectives, on_device(): lax.all_to_all(sent.reshape(32, 8, CX), 'gz', split_axis=0, concat_axis=0...  16.2 us
    ppermute x5, starting transfers between devices, shifted(): return lax.ppermute(value, axis, pairs)  15.6 us
    ppermute x5, waiting for transfers between devices, shifted(): return lax.ppermute(value, axis, pairs)  4.63 us
    pallas_call x1, Pallas kernels, on_device(): call(inner, (padded, speed, rows, padded, padded), [HB, HB], [pltpu.Semap...  2.83 us
    pallas_call x1, Pallas kernels, on_device(): call(borders, (slab, slab, joined_shape, moments_shape), [SM] * 3 + [VM]...  2.5 us
    pallas_call x1, Pallas kernels, on_device(): call(middle, (padded, padded, slab, shaped((SH_ROWS + 16, CX), I16)), [VM...  2.33 us
    pallas_call x1, Pallas kernels, on_device(): call(lower, (padded, slab), [VM] * 7, (), {5: 0, 6: 1}, cycles=1000)  1.74 us
    pallas_call x1, Pallas kernels, on_device(): call(finish, shaped((4, 4, CY), F32), [SM, VM], [pltpu.VMEM((256, CX), F3...  1.35 us
  transfers between devices with their start and end apart: 5, of which 2 were waited for; matrix products, arithmetic and copies ran while one was open for 0% of the time, Pallas kernels for 19%

profile of v2, /device:TPU:97, one launch (start us, length us, event | category | flops | bytes accessed | tf_op | source)
XLA Modules:
  0.0 50.7 jit_solution(18385882444315512036)
XLA Ops:
  0.6 1.1 %shard_map.95 = (bf16[768,128]{1,0:T(8,128)(2,1)S(1)}, bf16[768,128]{1,0:T(8,128)(2,1)S(1)}) custom-call(f32[2048,128]{1,0:T(8,128)} %bitcast.7, bf16[3,32,64,128]{3,2,1,0:T(8,128)(2,1)} %u_ref.3), custom_call_target="tpu_custom_call" | custom-call | flops 4096000 | bytes 1024000 | tf_op jit(solution)/shard_map/pallas_call | solution.py:416
  1.7 3.7 %collective-permute-start = (bf16[768,128]{1,0:T(8,128)(2,1)S(1)}, bf16[768,128]{1,0:T(8,128)(2,1)S(1)}, u32[]{:S(2)}, u32[]{:S(2)}) collective-permute-start(bf16[768,128]{1,0:T(8,128)(2,1)S(1)} %get-tuple-element.22), channel_id=1, source_target_pairs={{0,1},{1,2},{2,3},{3,4},{4,5},{5,6},{6,7},{7,8},{8,9},{9,10},{10,1... | collective-permute-start | bytes 589832 | tf_op jit(solution)/shard_map/ppermute | solution.py:49
  5.4 1.9 %collective-permute-start.1 = (bf16[768,128]{1,0:T(8,128)(2,1)S(1)}, bf16[768,128]{1,0:T(8,128)(2,1)S(1)}, u32[]{:S(2)}, u32[]{:S(2)}) collective-permute-start(bf16[768,128]{1,0:T(8,128)(2,1)S(1)} %get-tuple-element.23), channel_id=1, source_target_pairs={{1,0},{2,1},{3,2},{4,3},{5,4},{6,5},{7,6},{8,7},{9,8},{10,9},{11,1... | collective-permute-start | bytes 589832 | tf_op jit(solution)/shard_map/ppermute | solution.py:49
  7.3 2.8 %shard_map.96 = (f32[2576,128]{1,0:T(8,128)S(1)}, bf16[3,32,64,128]{3,2,1,0:T(8,128)(2,1)S(1)}, f32[1920,128]{1,0:T(8,128)S(1)}, f32[2576,128]{1,0:T(8,128)S(1)}, f32[2576,128]{1,0:T(8,128)S(1)}) custom-call(f32[2048,128]{1,0:T(8,128)} %bitcast.8, bf16[3,32,64,128]{3,2,1,0:T(8,128)(2,1)} %u_ref.3), custom_call_target="tpu_custom_call" | custom-call | flops 12288000 | bytes 3072000 | tf_op jit(solution)/shard_map/pallas_call | solution.py:426
  10.2 0.0 collective-permute-done.below_ref
  10.2 2.2 %collective-permute-done.1.above_ref = bf16[768,128]{1,0:T(8,128)(2,1)S(1)} collective-permute-done((bf16[768,128]{1,0:T(8,128)(2,1)S(1)}, bf16[768,128]{1,0:T(8,128)(2,1)S(1)}, u32[]{:S(2)}, u32[]{:S(2)}) %collective-permute-start.1) | collective-permute-done | bytes 196640 | tf_op jit(solution)/shard_map/ppermute | solution.py:49
  12.4 0.0 copy-start
  12.4 0.2 shard_map.97
  12.6 4.8 %collective-permute-start.2 = (bf16[1088,128]{1,0:T(8,128)(2,1)S(1)}, bf16[1088,128]{1,0:T(8,128)(2,1)S(1)}, u32[]{:S(2)}, u32[]{:S(2)}) collective-permute-start(bf16[1088,128]{1,0:T(8,128)(2,1)S(1)} %get-tuple-element.28), channel_id=1, source_target_pairs={{0,32},{32,64},{64,96},{96,128},{128,160},{160,192},{192,224},{1,3... | collective-permute-start | bytes 835592 | tf_op jit(solution)/shard_map/ppermute | solution.py:49
  17.4 0.0 copy-done
  17.4 2.3 %shard_map.98 = (f32[2576,128]{1,0:T(8,128)S(1)}, f32[2576,128]{1,0:T(8,128)S(1)}, f32[2048,128]{1,0:T(8,128)S(1)}, s16[976,128]{1,0:T(8,128)(2,1)S(1)}) custom-call(f32[128,128]{1,0:T(8,128)S(1)} %copy-done, bf16[3,32,64,128]{3,2,1,0:T(8,128)(2,1)S(1)} %get-tuple-element.30.u_ref, ...), custom_call_target="tpu_custom_call", output_to_operand_aliasing={{0}: (5, {}), {1}: (6, {})} | custom-call | flops 10240000 | bytes 2560000 | tf_op jit(solution)/shard_map/pallas_call | solution.py:440
  19.7 2.6 %collective-permute-start.4 = (s16[976,128]{1,0:T(8,128)(2,1)S(1)}, s16[976,128]{1,0:T(8,128)(2,1)S(1)}, u32[]{:S(2)}, u32[]{:S(2)}) collective-permute-start(s16[976,128]{1,0:T(8,128)(2,1)S(1)} %get-tuple-element.38), channel_id=1, source_target_pairs={{0,32},{32,64},{64,96},{96,128},{128,160},{160,192},{192,224},{1,3... | collective-permute-start | bytes 749576 | tf_op jit(solution)/shard_map/ppermute | solution.py:49
  22.4 2.6 %collective-permute-start.3 = (bf16[480,128]{1,0:T(8,128)(2,1)S(1)}, bf16[480,128]{1,0:T(8,128)(2,1)S(1)}, u32[]{:S(2)}, u32[]{:S(2)}) collective-permute-start(bf16[480,128]{1,0:T(8,128)(2,1)S(1)} %get-tuple-element.29), channel_id=1, source_target_pairs={{32,0},{64,32},{96,64},{128,96},{160,128},{192,160},{224,192},{33,... | collective-permute-start | bytes 368648 | tf_op jit(solution)/shard_map/ppermute | solution.py:49
  25.0 0.0 copy-start.1
  25.0 0.0 copy-start.2
  25.1 0.0 copy-start.3
  25.1 1.7 %shard_map.99 = (f32[2576,128]{1,0:T(8,128)S(1)}, f32[2048,128]{1,0:T(8,128)S(1)}) custom-call(bf16[3,32,64,128]{3,2,1,0:T(8,128)(2,1)S(1)} %get-tuple-element.30.u_ref, bf16[768,128]{1,0:T(8,128)(2,1)S(1)} %collective-permute-done.below_ref, bf16[768,128]{1,0:T(8,128)(2,1)S(1)} %collective-permute-done.1.above_ref, ...), custom_call_target="tpu_custom_call", output_to_operand_aliasing={{0}: (5, {}), {1}: (6, {})} | custom-call | flops 4096000 | bytes 1024000 | tf_op jit(solution)/shard_map/pallas_call | solution.py:451
  26.8 2.4 %collective-permute-done.3.above_ref = bf16[480,128]{1,0:T(8,128)(2,1)S(1)} collective-permute-done((bf16[480,128]{1,0:T(8,128)(2,1)S(1)}, bf16[480,128]{1,0:T(8,128)(2,1)S(1)}, u32[]{:S(2)}, u32[]{:S(2)}) %collective-permute-start.3) | collective-permute-done | bytes 122912 | tf_op jit(solution)/shard_map/ppermute | solution.py:49
  29.2 0.0 collective-permute-done.2.below_ref
  29.2 0.0 copy-done.1
  29.2 0.0 copy-done.2
  29.2 0.0 copy-done.3
  29.2 0.0 copy-start.4
  29.3 2.5 %shard_map.100 = (f32[2048,128]{1,0:T(8,128)S(1)}, f32[2048,128]{1,0:T(8,128)}, f32[2560,128]{1,0:T(8,128)S(1)}, f32[320,128]{1,0:T(8,128)S(1)}) custom-call(s32[32]{0:T(128)S(1)} %copy-done.1, s32[32]{0:T(128)S(1)} %copy-done.2, f32[2]{0:T(128)S(1)} %copy-done.3, f32[2576,128]{1,0:T(8,128)S(1)} %get-tuple-element.26.ss_ref, ...), custom_call_target="tpu_custom_call", output_to_operand_aliasing={{0}: (7, {})} | custom-call | flops 10240000 | bytes 2560000 | tf_op jit(solution)/shard_map/pallas_call | solution.py:454
  31.8 0.0 copy-start.5
  31.8 0.0 collective-permute-done.4.shear_ref
  31.8 0.0 copy-done.4
  31.8 1.3 %shard_map.101 = (f32[256,128]{1,0:T(8,128)S(1)}, f32[2560,128]{1,0:T(8,128)S(1)}, f32[320,128]{1,0:T(8,128)S(1)}) custom-call(s32[32]{0:T(128)S(1)} %copy-done.1, s32[32]{0:T(128)S(1)} %copy-done.2, f32[3,4]{1,0:T(4,128)S(1)} %copy-done.4, f32[2]{0:T(128)S(1)} %copy-done.3, f32[128,128]{1,0:T(8,128)S(1)} %copy-done, ...), custom_call_target="tpu_custom_call", output_to_operand_aliasing={{1}: (6, {}), {2}: (7, {})} | custom-call | flops 4096000 | bytes 1024000 | tf_op jit(solution)/shard_map/pallas_call | solution.py:463
  33.1 16.2 %all_to_all.5 = f32[32,8,128]{2,1,0:T(8,128)S(1)} all-to-all(f32[32,8,128]{2,1,0:T(8,128)S(1)} %bitcast.6), channel_id=1, replica_groups=mesh['gy'=8,'gz'=32] {'gz'}, dimensions={0} | all-to-all | bytes 262144 | tf_op jit(solution)/shard_map/all_to_all | solution.py:470
  49.3 0.0 copy-done.5
  49.3 1.4 %shard_map.102 = f32[4,4,64]{2,1,0:T(4,128)} custom-call(s32[32]{0:T(128)S(1)} %copy-done.5, f32[256,128]{1,0:T(8,128)S(1)} %bitcast.5), custom_call_target="tpu_custom_call" | custom-call | flops 4096000 | bytes 1024000 | tf_op jit(solution)/shard_map/pallas_call | solution.py:472
Async XLA Ops:
  1.7 8.5 %collective-permute-start = (bf16[768,128]{1,0:T(8,128)(2,1)S(1)}, bf16[768,128]{1,0:T(8,128)(2,1)S(1)}, u32[]{:S(2)}, u32[]{:S(2)}) collective-permute-start(bf16[768,128]{1,0:T(8,128)(2,1)S(1)} %get-tuple-element.22), channel_id=1, source_target_pairs={{0,1},{1,2},{2,3},{3,4},{4,5},{5,6},{6,7},{7,8},{8,9},{9,10},{10,1... | collective-permute-start | bytes 589832 | tf_op jit(solution)/shard_map/ppermute | solution.py:49
  5.4 7.0 %collective-permute-start.1 = (bf16[768,128]{1,0:T(8,128)(2,1)S(1)}, bf16[768,128]{1,0:T(8,128)(2,1)S(1)}, u32[]{:S(2)}, u32[]{:S(2)}) collective-permute-start(bf16[768,128]{1,0:T(8,128)(2,1)S(1)} %get-tuple-element.23), channel_id=1, source_target_pairs={{1,0},{2,1},{3,2},{4,3},{5,4},{6,5},{7,6},{8,7},{9,8},{10,9},{11,1... | collective-permute-start | bytes 589832 | tf_op jit(solution)/shard_map/ppermute | solution.py:49
  12.4 5.0 %copy-start = (f32[128,128]{1,0:T(8,128)S(1)}, f32[128,128]{1,0:T(8,128)}, u32[]{:S(2)}) copy-start(f32[128,128]{1,0:T(8,128)} %constant.2.clone.pow_ref) | copy-start | bytes 196612
  12.6 16.6 %collective-permute-start.2 = (bf16[1088,128]{1,0:T(8,128)(2,1)S(1)}, bf16[1088,128]{1,0:T(8,128)(2,1)S(1)}, u32[]{:S(2)}, u32[]{:S(2)}) collective-permute-start(bf16[1088,128]{1,0:T(8,128)(2,1)S(1)} %get-tuple-element.28), channel_id=1, source_target_pairs={{0,32},{32,64},{64,96},{96,128},{128,160},{160,192},{192,224},{1,3... | collective-permute-start | bytes 835592 | tf_op jit(solution)/shard_map/ppermute | solution.py:49
  19.7 12.0 %collective-permute-start.4 = (s16[976,128]{1,0:T(8,128)(2,1)S(1)}, s16[976,128]{1,0:T(8,128)(2,1)S(1)}, u32[]{:S(2)}, u32[]{:S(2)}) collective-permute-start(s16[976,128]{1,0:T(8,128)(2,1)S(1)} %get-tuple-element.38), channel_id=1, source_target_pairs={{0,32},{32,64},{64,96},{96,128},{128,160},{160,192},{192,224},{1,3... | collective-permute-start | bytes 749576 | tf_op jit(solution)/shard_map/ppermute | solution.py:49
  22.4 6.8 %collective-permute-start.3 = (bf16[480,128]{1,0:T(8,128)(2,1)S(1)}, bf16[480,128]{1,0:T(8,128)(2,1)S(1)}, u32[]{:S(2)}, u32[]{:S(2)}) collective-permute-start(bf16[480,128]{1,0:T(8,128)(2,1)S(1)} %get-tuple-element.29), channel_id=1, source_target_pairs={{32,0},{64,32},{96,64},{128,96},{160,128},{192,160},{224,192},{33,... | collective-permute-start | bytes 368648 | tf_op jit(solution)/shard_map/ppermute | solution.py:49
  25.0 4.2 %copy-start.1 = (s32[32]{0:T(128)S(1)}, s32[32]{0:T(128)}, u32[]{:S(2)}) copy-start(s32[32]{0:T(128)} %shift_ref.3) | copy-start | bytes 388
  25.0 4.2 %copy-start.2 = (s32[32]{0:T(128)S(1)}, s32[32]{0:T(128)}, u32[]{:S(2)}) copy-start(s32[32]{0:T(128)} %frac_ref.3) | copy-start | bytes 388
  25.1 4.2 %copy-start.3 = (f32[2]{0:T(128)S(1)}, f32[2]{0:T(128)}, u32[]{:S(2)}) copy-start(f32[2]{0:T(128)} %ext_ref.3) | copy-start | bytes 28
  29.2 2.5 %copy-start.4 = (f32[3,4]{1,0:T(4,128)S(1)}, f32[3,4]{1,0:T(4,128)}, u32[]{:S(2)}) copy-start(f32[3,4]{1,0:T(4,128)} %color_ref.1) | copy-start | bytes 148
  31.8 17.6 %copy-start.5 = (s32[32]{0:T(128)S(1)}, s32[32]{0:T(128)}, u32[]{:S(2)}) copy-start(s32[32]{0:T(128)} %rank_ref.1) | copy-start | bytes 388

commit v3 on v2

v3 whole, which is shorter than its diff:
```python
import jax
import jax.numpy as jnp
import numpy as np
from jax import lax
from jax.experimental import pallas as pl
from jax.experimental.pallas import tpu as pltpu
from jax.sharding import PartitionSpec as P


NFRAC = 8
SHIFT_MAX = 32
CZ, CY, CX = 32, 64, 128
PZ = 40
PLANE = CY
SS_ROWS = PZ * PLANE + 16
CELLS = CZ * CY
VV_PLANE = PZ * PLANE
J_ROWS = 80
UP, DOWN = 6, 3
UP_ROWS, DOWN_ROWS = 1088, 480
TOP = SHIFT_MAX + 1 - 3
SH_ROWS = CZ * TOP
F32, BF16, I16 = jnp.float32, jnp.bfloat16, jnp.int16
VM = pl.BlockSpec(memory_space=pltpu.VMEM)
SM = pl.BlockSpec(memory_space=pltpu.SMEM)
HB = pl.BlockSpec(memory_space=pltpu.HBM)


def call(kernel, outs, ins, scratch=(), aliases=None, out_specs=None, cycles=1000, vmem=16777216):
    return pl.pallas_call(
        kernel,
        out_shape=outs,
        in_specs=list(ins),
        out_specs=out_specs or jax.tree.map(lambda _: VM, outs),
        scratch_shapes=list(scratch),
        input_output_aliases=aliases or {},
        compiler_params=pltpu.CompilerParams(vmem_limit_bytes=vmem),
        cost_estimate=pl.CostEstimate(flops=4096 * cycles, bytes_accessed=1024 * cycles, transcendentals=0),
    )


def shaped(shape, dtype):
    return jax.ShapeDtypeStruct(shape, dtype)


def shifted(value, axis, by):
    count = lax.axis_size(axis)
    return lax.ppermute(value, axis, [(i, (i + by) % count) for i in range(count)])


def chained(value, axis, by):
    count = lax.axis_size(axis)
    return lax.ppermute(value, axis, [(i, i + by) for i in range(count) if 0 <= i + by < count])


def swapped(value, axis, first):
    count = lax.axis_size(axis)
    pairs = [(i, (i + 1) % count) for i in range(first, count, 2)]
    return lax.ppermute(value, axis, pairs + [(b, a) for a, b in pairs])


def split(value):
    high = value.astype(BF16)
    return high, (value - high.astype(F32)).astype(BF16)


def powers_of_two():
    return jnp.asarray(np.repeat((2.0 ** (np.arange(128) - 110.0)).astype(np.float32)[:, None], CX, 1))


def pack_z(s_ref, u_ref, far_ref, near_ref, s_buf, u_buf, sem):
    odd = lax.axis_index("gz") % 2
    copies = []
    for side, top in enumerate((odd, 1 - odd)):
        s_lo = pl.multiple_of(top * (CZ - 3) * CY, CY)
        copies.append(pltpu.make_async_copy(s_ref.at[pl.ds(s_lo, 3 * CY)], s_buf.at[side], sem.at[2 * side]))
        copies.append(pltpu.make_async_copy(u_ref.at[:, pl.ds(top * (CZ - 2), 2)], u_buf.at[side], sem.at[2 * side + 1]))
    for copy in copies:
        copy.start()
    for side, out in enumerate((far_ref, near_ref)):
        copies[2 * side].wait()
        high, low = split(s_buf[side])
        out[0 : 3 * CY] = high
        out[3 * CY : 6 * CY] = low
        copies[2 * side + 1].wait()
        for comp in range(3):
            out[(6 + 2 * comp) * CY : (8 + 2 * comp) * CY] = u_buf[side, comp].reshape(2 * CY, CX)


def flat(z):
    return 8 + PLANE * (z + 4)


def aligned(x):
    return x if isinstance(x, int) else pl.multiple_of(x, 8)


def gain(c, zn, zp, yn, yp, vz, vy, vx, lane):
    xn = jnp.where(lane == CX - 1, 0.0, pltpu.roll(c, CX - 1, 1))
    xp = jnp.where(lane == 0, 0.0, pltpu.roll(c, 1, 1))
    total = (zn + zp) + (yn + yp) + (xn + xp)
    return total - (vz * (zn - zp) + vy * (yn - yp) + vx * (xn - xp))


def first_of(c, g):
    return 0.94 * c + 0.01 * g


def second_of(s, c, g):
    return 0.75 * s + (0.25 * 0.94 * c + 0.25 * 0.01 * g)


def field_of(s, c, g):
    return (1.0 / 3.0) * s + (2.0 / 3.0 * 0.94 * c + 2.0 / 3.0 * 0.01 * g)


FULL = ((0, 16), (16, 16), (32, 16), (48, 16))
UPPER = ((24, 8), (32, 16), (48, 16))
UPPER_2, LOWER_2 = ((16, 16), (32, 16), (48, 16)), ((0, 16),)
EARLY = 30
LOWER = ((0, 16), (16, 8))


def one_plane(src, z, v_of, put, chunks=FULL):
    base = aligned(flat(z))
    near = src.at[pl.ds(aligned(base - 8), CY + 16)]
    after = src.at[pl.ds(aligned(base + PLANE), CY)]
    before = src.at[pl.ds(aligned(base - PLANE), CY)]
    for k, n in chunks:
        lane = lax.broadcasted_iota(jnp.int32, (n, CX), 1)
        c = near[8 + k : 8 + k + n]
        g = gain(
            c,
            after[k : k + n],
            before[k : k + n],
            near[9 + k : 9 + k + n],
            near[7 + k : 7 + k + n],
            *[v_of(comp, k, n) for comp in range(3)],
            lane,
        )
        put(aligned(base + k), k, n, c, g)


def v_at(comp, z):
    return aligned(comp * VV_PLANE + PLANE * (z + 4))


def run_planes(lo, hi, step, body):
    trips = (hi - lo) // step

    def group(i, _):
        for n in range(step):
            body(lo + i * step + n)
        return 0

    lax.fori_loop(0, trips, group, 0)
    for z in range(lo + trips * step, hi):
        body(z)


def speeds(vv_ref, z):
    planes = [vv_ref.at[pl.ds(v_at(comp, z), CY)] for comp in range(3)]
    return lambda comp, k, n: planes[comp][k : k + n]


def put_first(f1):
    def put(at, k, n, c, g):
        f1[pl.ds(at, n)] = first_of(c, g)

    return put


def put_second(f2, ss_ref):
    def put(at, k, n, c, g):
        f2[pl.ds(at, n)] = second_of(ss_ref[pl.ds(at, n)], c, g)

    return put


def put_field(field_ref, ss_ref):
    def put(at, k, n, c, g):
        field_ref[pl.ds(aligned(at - flat(0)), n)] = field_of(ss_ref[pl.ds(at, n)], c, g)

    return put


GROUP = 8


def inner(s_ref, u_ref, ss_ref, vv_ref, f1, f2, uv_ref, sem):
    copies = []
    for c in range(CZ // GROUP):
        rows = GROUP * CY
        copies.append(
            (
                pltpu.make_async_copy(s_ref.at[pl.ds(c * rows, rows)], ss_ref.at[pl.ds(flat(0) + c * rows, rows)], sem.at[2 * c]),
                pltpu.make_async_copy(u_ref.at[:, pl.ds(c * GROUP, GROUP)], uv_ref.at[:, pl.ds(c * GROUP, GROUP)], sem.at[2 * c + 1]),
            )
        )
    for pair in copies:
        for copy in pair:
            copy.start()

    def fresh(z):
        planes = [vv_ref.at[pl.ds(v_at(comp, z), CY)] for comp in range(3)]

        def of(comp, k, n):
            value = 10.0 * uv_ref[comp, z, k : k + n, :].astype(F32)
            planes[comp][k : k + n] = value
            return value

        return of

    for c, pair in enumerate(copies):
        for copy in pair:
            copy.wait()
        lo, hi = max(1, GROUP * c - 1), GROUP * (c + 1) - 1
        run_planes(lo, hi, 4, lambda z: one_plane(ss_ref, z, fresh(z), put_first(f1)))
    for z in (0, CZ - 1):
        of = fresh(z)
        for comp in range(3):
            for k, n in FULL:
                of(comp, k, n)
    run_planes(2, EARLY, 4, lambda z: one_plane(f1, z, speeds(vv_ref, z), put_second(f2, ss_ref), UPPER_2))


def inside(axis, side):
    place = lax.axis_index(axis)
    return jnp.where(place == (lax.axis_size(axis) - 1) * side, 0.0, 1.0)


def assemble(far_ref, near_ref, ss_in, vv_in, ss_ref, vv_ref, up_ref, down_ref, face):
    odd = lax.axis_index("gz") % 2 == 1

    def halo(side, plane, count):
        rows = slice(plane * CY, (plane + count) * CY)
        far, near = far_ref[rows].astype(F32), near_ref[rows].astype(F32)
        return jnp.where(odd, near, far) if side == 0 else jnp.where(odd, far, near)

    for side, z in ((0, -3), (1, CZ)):
        for n in range(3):
            ss_ref[flat(z + n) : flat(z + n) + CY] = (halo(side, n, 1) + halo(side, 3 + n, 1)) * inside("gz", side)
    for side, z in ((0, -2), (1, CZ)):
        for comp in range(3):
            for n in range(2):
                base = v_at(comp, z + n)
                vv_ref[base : base + CY] = 10.0 * halo(side, 6 + 2 * comp + n, 1)
    for out, count, s_lo, v_lo in ((up_ref, UP, CY - UP, CY - UP + 1), (down_ref, DOWN, 0, 0)):
        for row in range(count):
            value = ss_ref[pl.ds(8 + s_lo + row, PZ, stride=PLANE)]
            high = value.astype(BF16).astype(F32)
            face[row * PZ : (row + 1) * PZ] = high
            face[(count + row) * PZ : (count + row + 1) * PZ] = value - high
        for comp in range(3):
            for row in range(count - 1):
                at = 2 * count + (count - 1) * comp + row
                face[at * PZ : (at + 1) * PZ] = 0.1 * vv_ref[pl.ds(comp * VV_PLANE + v_lo + row, PZ, stride=PLANE)]
        out[...] = face[0 : out.shape[0]].astype(BF16)


def middle(pow_ref, vv_ref, ss_ref, f1_in, f2_in, f1, f2, field_ref, shear_ref, top):
    def mask(dst, width):
        for z, side in ((-width, 0), (CZ, 1)):
            rows = slice(flat(z), flat(z) + width * CY)
            dst[rows] = dst[rows] * inside("gz", side)

    for z in (-2, -1, 0, CZ - 1, CZ, CZ + 1):
        one_plane(ss_ref, z, speeds(vv_ref, z), put_first(f1))
    mask(f1, 2)
    for z in (-1, 0, 1, EARLY, EARLY + 1, CZ):
        one_plane(f1, z, speeds(vv_ref, z), put_second(f2, ss_ref), UPPER_2)
    mask(f2, 1)
    run_planes(0, CZ, 4, lambda z: one_plane(f2, z, speeds(vv_ref, z), put_field(field_ref, ss_ref), UPPER))
    for z in range(CZ):
        top[z * TOP : (z + 1) * TOP] = field_ref[z * CY + CY - TOP - 3 : (z + 1) * CY - 3]
    peak = jnp.max(jnp.abs(top[...]), axis=0, keepdims=True)
    enough = pow_ref[...] >= peak
    scale = jnp.min(jnp.where(enough, pow_ref[...], 2.0**17), axis=0, keepdims=True)
    step = jnp.sum(jnp.where(enough, 0.0, 1.0), axis=0, keepdims=True)
    shear_ref[0:SH_ROWS] = jnp.round(top[...] * (32000.0 / scale)).astype(I16)
    shear_ref[SH_ROWS : SH_ROWS + 16] = jnp.broadcast_to(step, (16, CX)).astype(I16)


def fix_rows(side, ss_ref, vv_ref, halo, field_ref, joined, face, se, fe, ge):
    count = (UP, DOWN)[side]
    first_own, first_halo, y_own, total = ((UP, 0, 0, UP + 6), (0, 6, CY - 6, 6 + DOWN))[side]
    lane = lax.broadcasted_iota(jnp.int32, (PZ, CX), 1)
    spot = lax.broadcasted_iota(jnp.int32, (PZ, CX), 0)
    z_mask = jnp.where(spot < 4, inside("gz", 0), jnp.where(spot >= 4 + CZ, inside("gz", 1), 1.0))
    y_mask = z_mask * inside("gy", side)
    face[0 : halo.shape[0]] = halo[...].astype(F32)

    def at(row):
        return 8 + row * PZ

    def beyond(row):
        return not first_own <= row < first_own + 6

    for n in range(6):
        r = at(first_own + n)
        se[r : r + PZ] = ss_ref[pl.ds(8 + y_own + n, PZ, stride=PLANE)]
    for n in range(count):
        r = at(first_halo + n)
        value = face[n * PZ : (n + 1) * PZ] + face[(count + n) * PZ : (count + n + 1) * PZ]
        se[r : r + PZ] = value * inside("gy", side)

    def velocity(comp, row):
        if not beyond(row):
            return vv_ref[pl.ds(comp * VV_PLANE + y_own + row - first_own, PZ, stride=PLANE)]
        q = (2 * count + (count - 1) * comp + (row - 1 if side == 0 else row - 6)) * PZ
        return 10.0 * face[q : q + PZ]

    def stage(src, row, of, *base):
        r = at(row)
        c = src[r : r + PZ]
        g = gain(
            c,
            src[r + 1 : r + 1 + PZ],
            src[r - 1 : r - 1 + PZ],
            src[r + PZ : r + 2 * PZ],
            src[r - PZ : r],
            *[velocity(comp, row) for comp in range(3)],
            lane,
        )
        return of(*[b[r : r + PZ] for b in base], c, g)

    for row in range(1, total - 1):
        fe[at(row) : at(row) + PZ] = stage(se, row, first_of) * (y_mask if beyond(row) else z_mask)
    for row in range(2, total - 2):
        ge[at(row) : at(row) + PZ] = stage(fe, row, second_of, se) * (y_mask if beyond(row) else z_mask)
    for row in range(3, total - 3):
        value = stage(ge, row, field_of, se)[4 : 4 + CZ]
        if beyond(row):
            joined[pl.ds(40 + row - first_own, CZ, stride=J_ROWS)] = value * inside("gy", side)
        else:
            field_ref[pl.ds(y_own + row - first_own, CZ, stride=CY)] = value


FACE_ROWS = 12 * PZ + 16


LOG2E = 1.4426950408889634


def march(shift_ref, frac_ref, ext_ref, src, start, n, mom_ref, lo):
    quad = ext_ref[0] * (-LOG2E / 1024.0)
    const = ext_ref[1] * (-LOG2E / 1024.0)

    def one(z, state):
        trans, depth, m1, m2, m3 = state
        at = start(z) - shift_ref[z]
        weight = frac_ref[z].astype(F32) * (1.0 / NFRAC)
        near = src[pl.ds(at, n), :]
        far = src[pl.ds(at - 1, n), :]
        g = (1.0 - weight) * near + weight * far
        g2 = g * g
        power = quad * g2 + const
        left = trans * jnp.exp2(power)
        share = trans - left
        s1 = share * g
        s2 = share * g2
        return left, depth + power, m1 + s1, m2 + s2, m3 + s2 * g

    zero = jnp.zeros((n, CX), F32)
    trans, depth, m1, m2, m3 = lax.fori_loop(0, CZ, one, (zero + 1.0, zero, zero, zero, zero), unroll=4)
    for i, value in enumerate((1.0 - trans, m1, m2, m3, depth * (-1.0 / LOG2E))):
        mom_ref[i * CY + lo : i * CY + lo + n] = value


def lower(vv_ref, ss_ref, f1, f2_in, field_in, f2, field_ref):
    for z in (-1, CZ):
        one_plane(f1, z, speeds(vv_ref, z), put_second(f2, ss_ref), LOWER_2)
        rows = slice(flat(z), flat(z) + 16)
        f2[rows] = f2[rows] * inside("gz", int(z == CZ))
    run_planes(0, CZ, 8, lambda z: one_plane(f1, z, speeds(vv_ref, z), put_second(f2, ss_ref), LOWER_2))
    run_planes(0, CZ, 8, lambda z: one_plane(f2, z, speeds(vv_ref, z), put_field(field_ref, ss_ref), LOWER))


def borders(shift_ref, frac_ref, ext_ref, ss_ref, vv_ref, below_ref, above_ref, field_in,
            field_ref, joined, mom_ref, face, se, fe, ge):
    fix_rows(0, ss_ref, vv_ref, below_ref, field_ref, joined, face, se, fe, ge)
    fix_rows(1, ss_ref, vv_ref, above_ref, field_ref, joined, face, se, fe, ge)
    march(shift_ref, frac_ref, ext_ref, field_ref, lambda z: z * CY + 40, 24, mom_ref, 40)
    for z in range(CZ):
        joined[z * J_ROWS + 40 : z * J_ROWS + 80] = field_ref[z * CY : z * CY + 40]


def lights(shift_ref, frac_ref, color_ref, ext_ref, pow_ref, shear_ref, field_ref, joined_in, mom_in,
           out_ref, joined, mom_ref, field_out_ref, above, turned, sem):
    copy = pltpu.make_async_copy(field_ref, field_out_ref, sem)
    copy.start()
    step = shear_ref[SH_ROWS : SH_ROWS + 16].astype(F32)[0:1]
    index = lax.broadcasted_iota(jnp.int32, (128, CX), 0).astype(F32)
    scale = jnp.sum(jnp.where(index == step, pow_ref[...], 0.0), axis=0, keepdims=True)
    above[...] = shear_ref[0:SH_ROWS].astype(F32) * (scale * (inside("gy", 0) * (1.0 / 32000.0)))
    for z in range(CZ):
        joined[z * J_ROWS + 7 : z * J_ROWS + 37] = above[z * TOP : (z + 1) * TOP]
    march(shift_ref, frac_ref, ext_ref, joined, lambda z: z * J_ROWS + 40, 40, mom_ref, 0)
    moments = [mom_ref[i * CY : (i + 1) * CY] for i in range(5)]
    for c in range(3):
        turned[c * CY : (c + 1) * CY] = (color_ref[c, 0] * moments[0] + color_ref[c, 1] * moments[1]) + (
            color_ref[c, 2] * moments[2] + color_ref[c, 3] * moments[3]
        )
    turned[3 * CY : 4 * CY] = moments[4]
    for h in range(2):
        turned[h * 128 : (h + 1) * 128] = turned[h * 128 : (h + 1) * 128].T
    for d in range(32):
        for h in range(2):
            out_ref[8 * d + 4 * h : 8 * d + 4 * h + 4] = turned[h * 128 + 4 * d : h * 128 + 4 * d + 4]
    copy.wait()


def finish(rank_ref, got_ref, image_ref, dep, order):
    for k in range(32):
        order[rank_ref[k]] = k
    got = got_ref[...].reshape(32, 8, 128)
    lane = lax.broadcasted_iota(jnp.int32, (32, 8, 128), 2)
    row = lax.broadcasted_iota(jnp.int32, (32, 8, 128), 1)
    depth = jnp.where(lane >= 64, got, pltpu.roll(got, 64, 2))
    depth = jnp.where(row >= 4, depth, pltpu.roll(depth, 4, 1))
    dep[...] = depth.reshape(256, 128)
    run = jnp.zeros((8, 128), F32)
    total = jnp.zeros((8, 128), F32)
    for r in range(32):
        base = pl.multiple_of(order[r] * 8, 8)
        total = total + jnp.exp(-run) * got_ref[pl.ds(base, 8)]
        run = run + dep[pl.ds(base, 8)]
    total = jnp.where((row[0] >= 4) & (lane[0] >= 64), 1.0 - jnp.exp(-run), total)
    for c in range(4):
        h, half = divmod(c, 2)
        image_ref[c] = total[4 * h : 4 * h + 4, 64 * half : 64 * half + 64]


def on_device(scalar, velocity, row_shift, frac_index, brick_rank, color_coeffs, extinction):
    powers = powers_of_two()
    hbm_scalar = pltpu.with_memory_space_constraint(scalar.reshape(CELLS, CX), pltpu.HBM)
    hbm_velocity = pltpu.with_memory_space_constraint(velocity, pltpu.HBM)

    z_face = shaped((12 * CY, CX), BF16)
    to_far, to_near = call(
        pack_z,
        (z_face, z_face),
        [HB, HB],
        [pltpu.VMEM((2, 3 * CY, CX), F32), pltpu.VMEM((2, 3, 2, CY, CX), BF16), pltpu.SemaphoreType.DMA((4,))],
    )(hbm_scalar, hbm_velocity)
    far = swapped(to_far, "gz", 1)
    near = swapped(to_near, "gz", 0)

    padded, slab = shaped((SS_ROWS, CX), F32), shaped((CELLS, CX), F32)
    speed = shaped((3 * VV_PLANE, CX), F32)
    ss, vv, f1, f2 = call(
        inner,
        (padded, speed, padded, padded),
        [HB, HB],
        [pltpu.VMEM((3, CZ, CY, CX), BF16), pltpu.SemaphoreType.DMA((8,))],
        cycles=3000,
    )(hbm_scalar, hbm_velocity)

    ss, vv, y_up, y_down = call(
        assemble,
        (padded, speed, shaped((UP_ROWS, CX), BF16), shaped((DOWN_ROWS, CX), BF16)),
        [VM] * 4,
        [pltpu.VMEM((UP_ROWS, CX), F32)],
        {2: 0, 3: 1},
    )(far, near, ss, vv)
    y_below = shifted(y_up, "gy", 1)
    y_above = shifted(y_down, "gy", -1)

    f1, f2, field, top = call(
        middle,
        (padded, padded, slab, shaped((SH_ROWS + 16, CX), I16)),
        [VM] * 5,
        [pltpu.VMEM((SH_ROWS, CX), F32)],
        {3: 0, 4: 1},
        cycles=2500,
    )(powers, vv, ss, f1, f2)
    above = chained(top, "gy", 1)

    joined_shape, moments_shape = shaped((CZ * J_ROWS, CX), F32), shaped((5 * CY, CX), F32)
    _, field = call(lower, (padded, slab), [VM] * 5, (), {3: 0, 4: 1}, cycles=1000)(vv, ss, f1, f2, field)
    field, joined, moments = call(
        borders,
        (slab, joined_shape, moments_shape),
        [SM] * 3 + [VM] * 5,
        [pltpu.VMEM((UP_ROWS, CX), F32)] + [pltpu.VMEM((FACE_ROWS, CX), F32)] * 3,
        {7: 0},
        cycles=2500,
    )(row_shift, frac_index, extinction, ss, vv, y_below, y_above, field)
    sent, _, _, field_out = call(
        lights,
        (shaped((256, CX), F32), joined_shape, moments_shape, slab),
        [SM] * 4 + [VM] * 5,
        [pltpu.VMEM((SH_ROWS, CX), F32), pltpu.VMEM((256, CX), F32), pltpu.SemaphoreType.DMA],
        {7: 1, 8: 2},
        (VM, VM, VM, HB),
    )(row_shift, frac_index, color_coeffs, extinction, powers, above, field, joined, moments)
    got = lax.all_to_all(sent.reshape(32, 8, CX), "gz", split_axis=0, concat_axis=0, tiled=True)

    image = call(
        finish,
        shaped((4, 4, CY), F32),
        [SM, VM],
        [pltpu.VMEM((256, CX), F32), pltpu.SMEM((32,), jnp.int32)],
    )(brick_rank, got.reshape(256, CX))
    return field_out.reshape(CZ, CY, CX), jnp.transpose(image, (0, 2, 1))


def solution(mesh):
    placed = (P("gz", "gy", None), P(None, "gz", "gy", None), P("gz"), P("gz"), P(), P(), P())
    return jax.shard_map(
        on_device,
        mesh=mesh,
        in_specs=placed,
        out_specs=(P("gz", "gy", None), P(None, "gy", "gz")),
        check_vma=False,
    )
```

time: 51 us -> 43.2 us (0.85)
  starting transfers between devices: 15.6 us -> 11.8 us
  blocking collectives: 16.2 us -> 13.9 us
  waiting for transfers between devices: 4.63 us -> 3.14 us
    ppermute x5, starting transfers between devices: 15.6 us -> 11.8 us  [the longest x2 5.41 us: swapped(): return lax.ppermute(value, axis, pairs + [(b, a) for a, b in pairs])]
    all_to_all x1, blocking collectives: 16.2 us -> 13.9 us  [on_device(): lax.all_to_all(sent.reshape(32, 8, CX), 'gz', split_axis=0, concat_axis=0...]
    ppermute x5, waiting for transfers between devices: 4.63 us -> 3.14 us  [the longest x2 3.14 us: shifted(): lax.ppermute(value, axis, [(i, (i + by) % count) for i in range(count)])]
    pallas_call x1, Pallas kernels: 2.33 us -> 1.55 us  [on_device(): call(middle, (padded, padded, slab, shaped((SH_ROWS + 16, CX), I16)), [VM...]
    pallas_call x5, Pallas kernels: 8.6 us -> 9.35 us  [the longest x1 3.34 us: on_device(): call(inner, (padded, speed, padded, padded), [HB, HB], [pltpu.VMEM((3, CZ...]
  transfers between devices with their start and end apart: 5 -> 5, of which waited for: 2 -> 1; matrix products, arithmetic and copies ran while one was open for 0% -> 0% of each run, Pallas kernels for 19% -> 20%
where the time goes in v3:
time: 43.2 us; the launch traced here: 43 us
  blocking collectives  13.9 us (32%)
  Pallas kernels  13.3 us (31%)
  starting transfers between devices  11.8 us (27%)
  waiting for transfers between devices  3.14 us (7%)
  between operations  0.76 us (2%)
    all_to_all x1, blocking collectives, on_device(): lax.all_to_all(sent.reshape(32, 8, CX), 'gz', split_axis=0, concat_axis=0...  13.9 us
    ppermute x2, starting transfers between devices, swapped(): return lax.ppermute(value, axis, pairs + [(b, a) for a, b in pairs])  5.41 us
    ppermute x2, starting transfers between devices, shifted(): lax.ppermute(value, axis, [(i, (i + by) % count) for i in range(count)])  3.73 us
    pallas_call x1, Pallas kernels, on_device(): call(inner, (padded, speed, padded, padded), [HB, HB], [pltpu.VMEM((3, CZ...  3.34 us
    ppermute x2, waiting for transfers between devices, shifted(): lax.ppermute(value, axis, [(i, (i + by) % count) for i in range(count)])  3.14 us
    pallas_call x1, Pallas kernels, on_device(): call(borders, (slab, joined_shape, moments_shape), [SM] * 3 + [VM] * 5, [...  2.84 us
    ppermute x1, starting transfers between devices, chained(): lax.ppermute(value, axis, [(i, i + by) for i in range(count) if 0 <= i +...  2.65 us
    pallas_call x1, Pallas kernels, on_device(): call(lights, (shaped((256, CX), F32), joined_shape, moments_shape, slab),...  1.57 us
  transfers between devices with their start and end apart: 5, of which 1 were waited for; matrix products, arithmetic and copies ran while one was open for 0% of the time, Pallas kernels for 20%

profile of v3, /device:TPU:97, one launch (start us, length us, event | category | flops | bytes accessed | tf_op | source)
XLA Modules:
  0.0 43.0 jit_solution(8792314563299212823)
XLA Ops:
  0.6 1.1 %shard_map.95 = (bf16[768,128]{1,0:T(8,128)(2,1)S(1)}, bf16[768,128]{1,0:T(8,128)(2,1)S(1)}) custom-call(f32[2048,128]{1,0:T(8,128)} %bitcast.7, bf16[3,32,64,128]{3,2,1,0:T(8,128)(2,1)} %u_ref.3), custom_call_target="tpu_custom_call" | custom-call | flops 4096000 | bytes 1024000 | tf_op jit(solution)/shard_map/pallas_call | solution.py:440
  1.7 1.9 %collective-permute-start = (bf16[768,128]{1,0:T(8,128)(2,1)S(1)}, bf16[768,128]{1,0:T(8,128)(2,1)S(1)}, u32[]{:S(2)}, u32[]{:S(2)}) collective-permute-start(bf16[768,128]{1,0:T(8,128)(2,1)S(1)} %get-tuple-element.22), channel_id=1, source_target_pairs={{1,2},{3,4},{5,6},{7,8},{9,10},{11,12},{13,14},{15,16},{17,18},{19... | collective-permute-start | bytes 589832 | tf_op jit(solution)/shard_map/ppermute | solution.py:59
  3.6 3.6 %collective-permute-start.1 = (bf16[768,128]{1,0:T(8,128)(2,1)S(1)}, bf16[768,128]{1,0:T(8,128)(2,1)S(1)}, u32[]{:S(2)}, u32[]{:S(2)}) collective-permute-start(bf16[768,128]{1,0:T(8,128)(2,1)S(1)} %get-tuple-element.23), channel_id=1, source_target_pairs={{0,1},{2,3},{4,5},{6,7},{8,9},{10,11},{12,13},{14,15},{16,17},{18,... | collective-permute-start | bytes 589832 | tf_op jit(solution)/shard_map/ppermute | solution.py:59
  7.1 3.3 %shard_map.96 = (f32[2576,128]{1,0:T(8,128)S(1)}, f32[7680,128]{1,0:T(8,128)S(1)}, f32[2576,128]{1,0:T(8,128)S(1)}, f32[2576,128]{1,0:T(8,128)S(1)}) custom-call(f32[2048,128]{1,0:T(8,128)} %bitcast.8, bf16[3,32,64,128]{3,2,1,0:T(8,128)(2,1)} %u_ref.3), custom_call_target="tpu_custom_call" | custom-call | flops 12288000 | bytes 3072000 | tf_op jit(solution)/shard_map/pallas_call | solution.py:451
  10.5 0.0 collective-permute-done.far_ref
  10.5 0.0 collective-permute-done.1.near_ref
  10.5 0.0 copy-start
  10.5 0.5 %shard_map.97 = (f32[2576,128]{1,0:T(8,128)S(1)}, f32[7680,128]{1,0:T(8,128)S(1)}, bf16[1088,128]{1,0:T(8,128)(2,1)S(1)}, bf16[480,128]{1,0:T(8,128)(2,1)S(1)}) custom-call(bf16[768,128]{1,0:T(8,128)(2,1)S(1)} %collective-permute-done.far_ref, bf16[768,128]{1,0:T(8,128)(2,1)S(1)} %collective-permute-done.1.near_ref, ...), custom_call_target="tpu_custom_call", output_to_operand_aliasing={{0}: (2, {}), {1}: (3, {})} | custom-call | flops 4096000 | bytes 1024000 | tf_op jit(solution)/shard_map/pallas_call | solution.py:459
  11.1 2.9 %collective-permute-start.3 = (bf16[1088,128]{1,0:T(8,128)(2,1)S(1)}, bf16[1088,128]{1,0:T(8,128)(2,1)S(1)}, u32[]{:S(2)}, u32[]{:S(2)}) collective-permute-start(bf16[1088,128]{1,0:T(8,128)(2,1)S(1)} %get-tuple-element.31), channel_id=1, source_target_pairs={{0,32},{32,64},{64,96},{96,128},{128,160},{160,192},{192,224},{224... | collective-permute-start | bytes 835592 | tf_op jit(solution)/shard_map/ppermute | solution.py:48
  14.0 0.0 copy-done
  14.0 1.6 %shard_map.98 = (f32[2576,128]{1,0:T(8,128)S(1)}, f32[2576,128]{1,0:T(8,128)S(1)}, f32[2048,128]{1,0:T(8,128)S(1)}, s16[976,128]{1,0:T(8,128)(2,1)S(1)}) custom-call(f32[128,128]{1,0:T(8,128)S(1)} %copy-done, f32[7680,128]{1,0:T(8,128)S(1)} %get-tuple-element.26.vv_ref, ...), custom_call_target="tpu_custom_call", output_to_operand_aliasing={{0}: (3, {}), {1}: (4, {})} | custom-call | flops 10240000 | bytes 2560000 | tf_op jit(solution)/shard_map/pallas_call | solution.py:469
  15.5 2.6 %collective-permute-start.2 = (s16[976,128]{1,0:T(8,128)(2,1)S(1)}, s16[976,128]{1,0:T(8,128)(2,1)S(1)}, u32[]{:S(2)}, u32[]{:S(2)}) collective-permute-start(s16[976,128]{1,0:T(8,128)(2,1)S(1)} %get-tuple-element.30), channel_id=1, source_target_pairs={{0,32},{32,64},{64,96},{96,128},{128,160},{160,192},{192,224},{1,3... | collective-permute-start | bytes 749576 | tf_op jit(solution)/shard_map/ppermute | solution.py:53
  18.2 0.8 %collective-permute-start.4 = (bf16[480,128]{1,0:T(8,128)(2,1)S(1)}, bf16[480,128]{1,0:T(8,128)(2,1)S(1)}, u32[]{:S(2)}, u32[]{:S(2)}) collective-permute-start(bf16[480,128]{1,0:T(8,128)(2,1)S(1)} %get-tuple-element.32), channel_id=1, source_target_pairs={{0,224},{32,0},{64,32},{96,64},{128,96},{160,128},{192,160},{224,1... | collective-permute-start | bytes 368648 | tf_op jit(solution)/shard_map/ppermute | solution.py:48
  19.0 0.0 copy-start.2
  19.0 0.0 copy-start.3
  19.0 0.0 copy-start.4
  19.0 1.1 %shard_map.99 = (f32[2576,128]{1,0:T(8,128)S(1)}, f32[2048,128]{1,0:T(8,128)S(1)}) custom-call(f32[7680,128]{1,0:T(8,128)S(1)} %get-tuple-element.26.vv_ref, f32[2576,128]{1,0:T(8,128)S(1)} %get-tuple-element.27.ss_ref, f32[2576,128]{1,0:T(8,128)S(1)} %get-tuple-element.33.f1, ...), custom_call_target="tpu_custom_call", output_to_operand_aliasing={{0}: (3, {}), {1}: (4, {})} | custom-call | flops 4096000 | bytes 1024000 | tf_op jit(solution)/shard_map/pallas_call | solution.py:480
  20.1 3.1 %collective-permute-done.4.above_ref = bf16[480,128]{1,0:T(8,128)(2,1)S(1)} collective-permute-done((bf16[480,128]{1,0:T(8,128)(2,1)S(1)}, bf16[480,128]{1,0:T(8,128)(2,1)S(1)}, u32[]{:S(2)}, u32[]{:S(2)}) %collective-permute-start.4) | collective-permute-done | bytes 122912 | tf_op jit(solution)/shard_map/ppermute | solution.py:48
  23.2 0.0 collective-permute-done.3.below_ref
  23.2 0.0 copy-done.2
  23.2 0.0 copy-done.3
  23.2 0.0 copy-done.4
  23.2 0.0 copy-start.1
  23.3 2.8 %shard_map.100 = (f32[2048,128]{1,0:T(8,128)S(1)}, f32[2560,128]{1,0:T(8,128)S(1)}, f32[320,128]{1,0:T(8,128)S(1)}) custom-call(s32[32]{0:T(128)S(1)} %copy-done.2, s32[32]{0:T(128)S(1)} %copy-done.3, f32[2]{0:T(128)S(1)} %copy-done.4, f32[2576,128]{1,0:T(8,128)S(1)} %get-tuple-element.27.ss_ref, ...), custom_call_target="tpu_custom_call", output_to_operand_aliasing={{0}: (7, {})} | custom-call | flops 10240000 | bytes 2560000 | tf_op jit(solution)/shard_map/pallas_call | solution.py:481
  26.1 0.0 collective-permute-done.2.shear_ref
  26.1 0.0 copy-done.1
  26.1 0.0 copy-start.5
  26.1 1.6 %shard_map.101 = (f32[256,128]{1,0:T(8,128)S(1)}, f32[2560,128]{1,0:T(8,128)S(1)}, f32[320,128]{1,0:T(8,128)S(1)}, f32[2048,128]{1,0:T(8,128)}) custom-call(s32[32]{0:T(128)S(1)} %copy-done.2, s32[32]{0:T(128)S(1)} %copy-done.3, f32[3,4]{1,0:T(4,128)S(1)} %copy-done.1, f32[2]{0:T(128)S(1)} %copy-done.4, ...), custom_call_target="tpu_custom_call", output_to_operand_aliasing={{1}: (7, {}), {2}: (8, {})} | custom-call | flops 4096000 | bytes 1024000 | tf_op jit(solution)/shard_map/pallas_call | solution.py:489
  27.7 13.9 %all_to_all.5 = f32[32,8,128]{2,1,0:T(8,128)S(1)} all-to-all(f32[32,8,128]{2,1,0:T(8,128)S(1)} %bitcast.6), channel_id=1, replica_groups=mesh['gy'=8,'gz'=32] {'gz'}, dimensions={0} | all-to-all | bytes 262144 | tf_op jit(solution)/shard_map/all_to_all | solution.py:497
  41.6 0.0 copy-done.5
  41.6 1.4 %shard_map.102 = f32[4,4,64]{2,1,0:T(4,128)} custom-call(s32[32]{0:T(128)S(1)} %copy-done.5, f32[256,128]{1,0:T(8,128)S(1)} %bitcast.5), custom_call_target="tpu_custom_call" | custom-call | flops 4096000 | bytes 1024000 | tf_op jit(solution)/shard_map/pallas_call | solution.py:499
Async XLA Ops:
  1.7 8.8 %collective-permute-start = (bf16[768,128]{1,0:T(8,128)(2,1)S(1)}, bf16[768,128]{1,0:T(8,128)(2,1)S(1)}, u32[]{:S(2)}, u32[]{:S(2)}) collective-permute-start(bf16[768,128]{1,0:T(8,128)(2,1)S(1)} %get-tuple-element.22), channel_id=1, source_target_pairs={{1,2},{3,4},{5,6},{7,8},{9,10},{11,12},{13,14},{15,16},{17,18},{19... | collective-permute-start | bytes 589832 | tf_op jit(solution)/shard_map/ppermute | solution.py:59
  3.6 6.9 %collective-permute-start.1 = (bf16[768,128]{1,0:T(8,128)(2,1)S(1)}, bf16[768,128]{1,0:T(8,128)(2,1)S(1)}, u32[]{:S(2)}, u32[]{:S(2)}) collective-permute-start(bf16[768,128]{1,0:T(8,128)(2,1)S(1)} %get-tuple-element.23), channel_id=1, source_target_pairs={{0,1},{2,3},{4,5},{6,7},{8,9},{10,11},{12,13},{14,15},{16,17},{18,... | collective-permute-start | bytes 589832 | tf_op jit(solution)/shard_map/ppermute | solution.py:59
  10.5 3.5 %copy-start = (f32[128,128]{1,0:T(8,128)S(1)}, f32[128,128]{1,0:T(8,128)}, u32[]{:S(2)}) copy-start(f32[128,128]{1,0:T(8,128)} %constant.2.clone.pow_ref) | copy-start | bytes 196612
  11.1 12.2 %collective-permute-start.3 = (bf16[1088,128]{1,0:T(8,128)(2,1)S(1)}, bf16[1088,128]{1,0:T(8,128)(2,1)S(1)}, u32[]{:S(2)}, u32[]{:S(2)}) collective-permute-start(bf16[1088,128]{1,0:T(8,128)(2,1)S(1)} %get-tuple-element.31), channel_id=1, source_target_pairs={{0,32},{32,64},{64,96},{96,128},{128,160},{160,192},{192,224},{224... | collective-permute-start | bytes 835592 | tf_op jit(solution)/shard_map/ppermute | solution.py:48
  15.5 10.6 %collective-permute-start.2 = (s16[976,128]{1,0:T(8,128)(2,1)S(1)}, s16[976,128]{1,0:T(8,128)(2,1)S(1)}, u32[]{:S(2)}, u32[]{:S(2)}) collective-permute-start(s16[976,128]{1,0:T(8,128)(2,1)S(1)} %get-tuple-element.30), channel_id=1, source_target_pairs={{0,32},{32,64},{64,96},{96,128},{128,160},{160,192},{192,224},{1,3... | collective-permute-start | bytes 749576 | tf_op jit(solution)/shard_map/ppermute | solution.py:53
  18.2 5.0 %collective-permute-start.4 = (bf16[480,128]{1,0:T(8,128)(2,1)S(1)}, bf16[480,128]{1,0:T(8,128)(2,1)S(1)}, u32[]{:S(2)}, u32[]{:S(2)}) collective-permute-start(bf16[480,128]{1,0:T(8,128)(2,1)S(1)} %get-tuple-element.32), channel_id=1, source_target_pairs={{0,224},{32,0},{64,32},{96,64},{128,96},{160,128},{192,160},{224,1... | collective-permute-start | bytes 368648 | tf_op jit(solution)/shard_map/ppermute | solution.py:48
  19.0 4.2 %copy-start.2 = (s32[32]{0:T(128)S(1)}, s32[32]{0:T(128)}, u32[]{:S(2)}) copy-start(s32[32]{0:T(128)} %shift_ref.3) | copy-start | bytes 388
  19.0 4.2 %copy-start.3 = (s32[32]{0:T(128)S(1)}, s32[32]{0:T(128)}, u32[]{:S(2)}) copy-start(s32[32]{0:T(128)} %frac_ref.3) | copy-start | bytes 388
  19.0 4.2 %copy-start.4 = (f32[2]{0:T(128)S(1)}, f32[2]{0:T(128)}, u32[]{:S(2)}) copy-start(f32[2]{0:T(128)} %ext_ref.3) | copy-start | bytes 28
  23.2 2.9 %copy-start.1 = (f32[3,4]{1,0:T(4,128)S(1)}, f32[3,4]{1,0:T(4,128)}, u32[]{:S(2)}) copy-start(f32[3,4]{1,0:T(4,128)} %color_ref.1) | copy-start | bytes 148
  26.1 15.5 %copy-start.5 = (s32[32]{0:T(128)S(1)}, s32[32]{0:T(128)}, u32[]{:S(2)}) copy-start(s32[32]{0:T(128)} %rank_ref.1) | copy-start | bytes 388

commit v4 on v3

--- a/solution.py
+++ b/solution.py
@@ -17,7 +17,8 @@
 VV_PLANE = PZ * PLANE
 J_ROWS = 80
 UP, DOWN = 6, 3
-UP_ROWS, DOWN_ROWS = 1088, 480
+LOW = 3
+UP_ROWS, DOWN_ROWS = (UP + LOW + 15) * PZ, (DOWN + LOW + 6) * PZ
 TOP = SHIFT_MAX + 1 - 3
 SH_ROWS = CZ * TOP
 F32, BF16, I16 = jnp.float32, jnp.bfloat16, jnp.int16
@@ -250,10 +251,12 @@
             value = ss_ref[pl.ds(8 + s_lo + row, PZ, stride=PLANE)]
             high = value.astype(BF16).astype(F32)
             face[row * PZ : (row + 1) * PZ] = high
-            face[(count + row) * PZ : (count + row + 1) * PZ] = value - high
+            at = LOW + row
+            if at >= count:
+                face[at * PZ : (at + 1) * PZ] = value - high
         for comp in range(3):
             for row in range(count - 1):
-                at = 2 * count + (count - 1) * comp + row
+                at = count + LOW + (count - 1) * comp + row
                 face[at * PZ : (at + 1) * PZ] = 0.1 * vv_ref[pl.ds(comp * VV_PLANE + v_lo + row, PZ, stride=PLANE)]
         out[...] = face[0 : out.shape[0]].astype(BF16)
 
@@ -301,13 +304,15 @@
         se[r : r + PZ] = ss_ref[pl.ds(8 + y_own + n, PZ, stride=PLANE)]
     for n in range(count):
         r = at(first_halo + n)
-        value = face[n * PZ : (n + 1) * PZ] + face[(count + n) * PZ : (count + n + 1) * PZ]
+        value = face[n * PZ : (n + 1) * PZ]
+        if n >= count - LOW:
+            value = value + face[(LOW + n) * PZ : (LOW + n + 1) * PZ]
         se[r : r + PZ] = value * inside("gy", side)
 
     def velocity(comp, row):
         if not beyond(row):
             return vv_ref[pl.ds(comp * VV_PLANE + y_own + row - first_own, PZ, stride=PLANE)]
-        q = (2 * count + (count - 1) * comp + (row - 1 if side == 0 else row - 6)) * PZ
+        q = (count + LOW + (count - 1) * comp + (row - 1 if side == 0 else row - 6)) * PZ
         return 10.0 * face[q : q + PZ]
 
     def stage(src, row, of, *base):
@@ -376,11 +381,13 @@
     run_planes(0, CZ, 8, lambda z: one_plane(f2, z, speeds(vv_ref, z), put_field(field_ref, ss_ref), LOWER))
 
 
-def borders(shift_ref, frac_ref, ext_ref, ss_ref, vv_ref, below_ref, above_ref, field_in,
-            field_ref, joined, mom_ref, face, se, fe, ge):
+def high_rows(shift_ref, frac_ref, ext_ref, ss_ref, vv_ref, above_ref, field_in, field_ref, mom_ref, face, se, fe, ge):
+    fix_rows(1, ss_ref, vv_ref, above_ref, field_ref, None, face, se, fe, ge)
+    march(shift_ref, frac_ref, ext_ref, field_ref, lambda z: z * CY + 40, 24, mom_ref, 40)
+
+
+def low_rows(ss_ref, vv_ref, below_ref, field_in, field_ref, joined, face, se, fe, ge):
     fix_rows(0, ss_ref, vv_ref, below_ref, field_ref, joined, face, se, fe, ge)
-    fix_rows(1, ss_ref, vv_ref, above_ref, field_ref, joined, face, se, fe, ge)
-    march(shift_ref, frac_ref, ext_ref, field_ref, lambda z: z * CY + 40, 24, mom_ref, 40)
     for z in range(CZ):
         joined[z * J_ROWS + 40 : z * J_ROWS + 80] = field_ref[z * CY : z * CY + 40]
 
@@ -478,14 +485,13 @@
 
     joined_shape, moments_shape = shaped((CZ * J_ROWS, CX), F32), shaped((5 * CY, CX), F32)
     _, field = call(lower, (padded, slab), [VM] * 5, (), {3: 0, 4: 1}, cycles=1000)(vv, ss, f1, f2, field)
-    field, joined, moments = call(
-        borders,
-        (slab, joined_shape, moments_shape),
-        [SM] * 3 + [VM] * 5,
-        [pltpu.VMEM((UP_ROWS, CX), F32)] + [pltpu.VMEM((FACE_ROWS, CX), F32)] * 3,
-        {7: 0},
-        cycles=2500,
-    )(row_shift, frac_index, extinction, ss, vv, y_below, y_above, field)
+    scratch = [pltpu.VMEM((UP_ROWS, CX), F32)] + [pltpu.VMEM((FACE_ROWS, CX), F32)] * 3
+    field, moments = call(
+        high_rows, (slab, moments_shape), [SM] * 3 + [VM] * 4, scratch, {6: 0}, cycles=1500
+    )(row_shift, frac_index, extinction, ss, vv, y_above, field)
+    field, joined = call(low_rows, (slab, joined_shape), [VM] * 4, scratch, {3: 0}, cycles=1500)(
+        ss, vv, y_below, field
+    )
     sent, _, _, field_out = call(
         lights,
         (shaped((256, CX), F32), joined_shape, moments_shape, slab),

time: 43.2 us -> 45.3 us (1.049)
  the two profiles are of different devices: /device:TPU:97 before, /device:TPU:129 now
where the time goes in v4:
time: 45.3 us; the launch traced here: 45.1 us
  Pallas kernels  13.3 us (29%)
  blocking collectives  12.4 us (27%)
  starting transfers between devices  10.8 us (24%)
  waiting for transfers between devices  7.39 us (16%)
  between operations  0.75 us (2%)
    all_to_all x1, blocking collectives, on_device(): lax.all_to_all(sent.reshape(32, 8, CX), 'gz', split_axis=0, concat_axis=0...  12.4 us
    ppermute x2, waiting for transfers between devices, shifted(): lax.ppermute(value, axis, [(i, (i + by) % count) for i in range(count)])  7.38 us
    ppermute x2, starting transfers between devices, swapped(): return lax.ppermute(value, axis, pairs + [(b, a) for a, b in pairs])  5.41 us
    pallas_call x1, Pallas kernels, on_device(): call(inner, (padded, speed, padded, padded), [HB, HB], [pltpu.VMEM((3, CZ...  3.34 us
    ppermute x2, starting transfers between devices, shifted(): lax.ppermute(value, axis, [(i, (i + by) % count) for i in range(count)])  2.75 us
    ppermute x1, starting transfers between devices, chained(): lax.ppermute(value, axis, [(i, i + by) for i in range(count) if 0 <= i +...  2.65 us
    pallas_call x1, Pallas kernels, on_device(): call(high_rows, (slab, moments_shape), [SM] * 3 + [VM] * 4, scratch, {6:...  1.68 us
    pallas_call x1, Pallas kernels, on_device(): call(middle, (padded, padded, slab, shaped((SH_ROWS + 16, CX), I16)), [VM...  1.59 us
  transfers between devices with their start and end apart: 5, of which 2 were waited for; matrix products, arithmetic and copies ran while one was open for 0% of the time, Pallas kernels for 16%

profile of v4, /device:TPU:129, one launch (start us, length us, event | category | flops | bytes accessed | tf_op | source)
XLA Modules:
  0.0 45.1 jit_solution(8946743117816532305)
XLA Ops:
  0.6 1.1 %shard_map.95 = (bf16[768,128]{1,0:T(8,128)(2,1)S(1)}, bf16[768,128]{1,0:T(8,128)(2,1)S(1)}) custom-call(f32[2048,128]{1,0:T(8,128)} %bitcast.7, bf16[3,32,64,128]{3,2,1,0:T(8,128)(2,1)} %u_ref.3), custom_call_target="tpu_custom_call" | custom-call | flops 4096000 | bytes 1024000 | tf_op jit(solution)/shard_map/pallas_call | solution.py:447
  1.7 1.9 %collective-permute-start = (bf16[768,128]{1,0:T(8,128)(2,1)S(1)}, bf16[768,128]{1,0:T(8,128)(2,1)S(1)}, u32[]{:S(2)}, u32[]{:S(2)}) collective-permute-start(bf16[768,128]{1,0:T(8,128)(2,1)S(1)} %get-tuple-element.23), channel_id=1, source_target_pairs={{1,2},{3,4},{5,6},{7,8},{9,10},{11,12},{13,14},{15,16},{17,18},{19... | collective-permute-start | bytes 589832 | tf_op jit(solution)/shard_map/ppermute | solution.py:60
  3.6 3.6 %collective-permute-start.1 = (bf16[768,128]{1,0:T(8,128)(2,1)S(1)}, bf16[768,128]{1,0:T(8,128)(2,1)S(1)}, u32[]{:S(2)}, u32[]{:S(2)}) collective-permute-start(bf16[768,128]{1,0:T(8,128)(2,1)S(1)} %get-tuple-element.24), channel_id=1, source_target_pairs={{0,1},{2,3},{4,5},{6,7},{8,9},{10,11},{12,13},{14,15},{16,17},{18,... | collective-permute-start | bytes 589832 | tf_op jit(solution)/shard_map/ppermute | solution.py:60
  7.1 3.3 %shard_map.96 = (f32[2576,128]{1,0:T(8,128)S(1)}, f32[7680,128]{1,0:T(8,128)S(1)}, f32[2576,128]{1,0:T(8,128)S(1)}, f32[2576,128]{1,0:T(8,128)S(1)}) custom-call(f32[2048,128]{1,0:T(8,128)} %bitcast.8, bf16[3,32,64,128]{3,2,1,0:T(8,128)(2,1)} %u_ref.3), custom_call_target="tpu_custom_call" | custom-call | flops 12288000 | bytes 3072000 | tf_op jit(solution)/shard_map/pallas_call | solution.py:458
  10.5 0.0 collective-permute-done.far_ref
  10.5 0.0 collective-permute-done.1.near_ref
  10.5 0.0 copy-start
  10.5 0.5 %shard_map.97 = (f32[2576,128]{1,0:T(8,128)S(1)}, f32[7680,128]{1,0:T(8,128)S(1)}, bf16[960,128]{1,0:T(8,128)(2,1)S(1)}, bf16[480,128]{1,0:T(8,128)(2,1)S(1)}) custom-call(bf16[768,128]{1,0:T(8,128)(2,1)S(1)} %collective-permute-done.far_ref, bf16[768,128]{1,0:T(8,128)(2,1)S(1)} %collective-permute-done.1.near_ref, ...), custom_call_target="tpu_custom_call", output_to_operand_aliasing={{0}: (2, {}), {1}: (3, {})} | custom-call | flops 4096000 | bytes 1024000 | tf_op jit(solution)/shard_map/pallas_call | solution.py:466
  11.0 0.3 copy-done
  11.3 1.6 %shard_map.98 = (f32[2576,128]{1,0:T(8,128)S(1)}, f32[2576,128]{1,0:T(8,128)S(1)}, f32[2048,128]{1,0:T(8,128)S(1)}, s16[976,128]{1,0:T(8,128)(2,1)S(1)}) custom-call(f32[128,128]{1,0:T(8,128)S(1)} %copy-done, f32[7680,128]{1,0:T(8,128)S(1)} %get-tuple-element.27.vv_ref, ...), custom_call_target="tpu_custom_call", output_to_operand_aliasing={{0}: (3, {}), {1}: (4, {})} | custom-call | flops 10240000 | bytes 2560000 | tf_op jit(solution)/shard_map/pallas_call | solution.py:476
  12.9 2.6 %collective-permute-start.2 = (s16[976,128]{1,0:T(8,128)(2,1)S(1)}, s16[976,128]{1,0:T(8,128)(2,1)S(1)}, u32[]{:S(2)}, u32[]{:S(2)}) collective-permute-start(s16[976,128]{1,0:T(8,128)(2,1)S(1)} %get-tuple-element.31), channel_id=1, source_target_pairs={{0,32},{32,64},{64,96},{96,128},{128,160},{160,192},{192,224},{1,3... | collective-permute-start | bytes 749576 | tf_op jit(solution)/shard_map/ppermute | solution.py:54
  15.6 0.8 %collective-permute-start.3 = (bf16[960,128]{1,0:T(8,128)(2,1)S(1)}, bf16[960,128]{1,0:T(8,128)(2,1)S(1)}, u32[]{:S(2)}, u32[]{:S(2)}) collective-permute-start(bf16[960,128]{1,0:T(8,128)(2,1)S(1)} %get-tuple-element.32), channel_id=1, source_target_pairs={{0,32},{32,64},{64,96},{96,128},{128,160},{160,192},{192,224},{224... | collective-permute-start | bytes 737288 | tf_op jit(solution)/shard_map/ppermute | solution.py:49
  16.4 1.9 %collective-permute-start.4 = (bf16[480,128]{1,0:T(8,128)(2,1)S(1)}, bf16[480,128]{1,0:T(8,128)(2,1)S(1)}, u32[]{:S(2)}, u32[]{:S(2)}) collective-permute-start(bf16[480,128]{1,0:T(8,128)(2,1)S(1)} %get-tuple-element.33), channel_id=1, source_target_pairs={{0,224},{32,0},{64,32},{96,64},{128,96},{160,128},{192,160},{224,1... | collective-permute-start | bytes 368648 | tf_op jit(solution)/shard_map/ppermute | solution.py:49
  18.4 0.0 copy-start.2
  18.4 0.0 copy-start.3
  18.4 0.0 copy-start.4
  18.4 1.1 %shard_map.99 = (f32[2576,128]{1,0:T(8,128)S(1)}, f32[2048,128]{1,0:T(8,128)S(1)}) custom-call(f32[7680,128]{1,0:T(8,128)S(1)} %get-tuple-element.27.vv_ref, f32[2576,128]{1,0:T(8,128)S(1)} %get-tuple-element.28.ss_ref, f32[2576,128]{1,0:T(8,128)S(1)} %get-tuple-element.34.f1, ...), custom_call_target="tpu_custom_call", output_to_operand_aliasing={{0}: (3, {}), {1}: (4, {})} | custom-call | flops 4096000 | bytes 1024000 | tf_op jit(solution)/shard_map/pallas_call | solution.py:487
  19.4 1.0 %collective-permute-done.4.above_ref = bf16[480,128]{1,0:T(8,128)(2,1)S(1)} collective-permute-done((bf16[480,128]{1,0:T(8,128)(2,1)S(1)}, bf16[480,128]{1,0:T(8,128)(2,1)S(1)}, u32[]{:S(2)}, u32[]{:S(2)}) %collective-permute-start.4) | collective-permute-done | bytes 122912 | tf_op jit(solution)/shard_map/ppermute | solution.py:49
  20.4 0.0 copy-done.2
  20.4 0.0 copy-done.3
  20.4 0.0 copy-done.4
  20.4 1.7 %shard_map.100 = (f32[2048,128]{1,0:T(8,128)S(1)}, f32[320,128]{1,0:T(8,128)S(1)}) custom-call(s32[32]{0:T(128)S(1)} %copy-done.2, s32[32]{0:T(128)S(1)} %copy-done.3, f32[2]{0:T(128)S(1)} %copy-done.4, f32[2576,128]{1,0:T(8,128)S(1)} %get-tuple-element.28.ss_ref, f32[7680,128]{1,0:T(8,128)S(1)} %get-tuple-element.27.vv_ref, ...), custom_call_target="tpu_custom_call", output_to_operand_aliasing={{0}: (6, {})} | custom-call | flops 6144000 | bytes 1536000 | tf_op jit(solution)/shard_map/pallas_call | solution.py:489
  22.1 6.4 %collective-permute-done.3.below_ref = bf16[960,128]{1,0:T(8,128)(2,1)S(1)} collective-permute-done((bf16[960,128]{1,0:T(8,128)(2,1)S(1)}, bf16[960,128]{1,0:T(8,128)(2,1)S(1)}, u32[]{:S(2)}, u32[]{:S(2)}) %collective-permute-start.3) | collective-permute-done | bytes 245792 | tf_op jit(solution)/shard_map/ppermute | solution.py:49
  28.5 0.0 copy-start.1
  28.5 1.1 %shard_map.101 = (f32[2048,128]{1,0:T(8,128)S(1)}, f32[2560,128]{1,0:T(8,128)S(1)}) custom-call(f32[2576,128]{1,0:T(8,128)S(1)} %get-tuple-element.28.ss_ref, f32[7680,128]{1,0:T(8,128)S(1)} %get-tuple-element.27.vv_ref, bf16[960,128]{1,0:T(8,128)(2,1)S(1)} %collective-permute-done.3.below_ref, ...), custom_call_target="tpu_custom_call", output_to_operand_aliasing={{0}: (3, {})} | custom-call | flops 6144000 | bytes 1536000 | tf_op jit(solution)/shard_map/pallas_call | solution.py:492
  29.7 0.0 collective-permute-done.2.shear_ref
  29.7 0.0 copy-done.1
  29.7 0.0 copy-start.5
  29.7 1.6 %shard_map.102 = (f32[256,128]{1,0:T(8,128)S(1)}, f32[2560,128]{1,0:T(8,128)S(1)}, f32[320,128]{1,0:T(8,128)S(1)}, f32[2048,128]{1,0:T(8,128)}) custom-call(s32[32]{0:T(128)S(1)} %copy-done.2, s32[32]{0:T(128)S(1)} %copy-done.3, f32[3,4]{1,0:T(4,128)S(1)} %copy-done.1, f32[2]{0:T(128)S(1)} %copy-done.4, ...), custom_call_target="tpu_custom_call", output_to_operand_aliasing={{1}: (7, {}), {2}: (8, {})} | custom-call | flops 4096000 | bytes 1024000 | tf_op jit(solution)/shard_map/pallas_call | solution.py:495
  31.3 12.4 %all_to_all.5 = f32[32,8,128]{2,1,0:T(8,128)S(1)} all-to-all(f32[32,8,128]{2,1,0:T(8,128)S(1)} %bitcast.6), channel_id=1, replica_groups=mesh['gy'=8,'gz'=32] {'gz'}, dimensions={0} | all-to-all | bytes 262144 | tf_op jit(solution)/shard_map/all_to_all | solution.py:503
  43.7 0.0 copy-done.5
  43.7 1.4 %shard_map.103 = f32[4,4,64]{2,1,0:T(4,128)} custom-call(s32[32]{0:T(128)S(1)} %copy-done.5, f32[256,128]{1,0:T(8,128)S(1)} %bitcast.5), custom_call_target="tpu_custom_call" | custom-call | flops 4096000 | bytes 1024000 | tf_op jit(solution)/shard_map/pallas_call | solution.py:505
Async XLA Ops:
  1.7 8.8 %collective-permute-start = (bf16[768,128]{1,0:T(8,128)(2,1)S(1)}, bf16[768,128]{1,0:T(8,128)(2,1)S(1)}, u32[]{:S(2)}, u32[]{:S(2)}) collective-permute-start(bf16[768,128]{1,0:T(8,128)(2,1)S(1)} %get-tuple-element.23), channel_id=1, source_target_pairs={{1,2},{3,4},{5,6},{7,8},{9,10},{11,12},{13,14},{15,16},{17,18},{19... | collective-permute-start | bytes 589832 | tf_op jit(solution)/shard_map/ppermute | solution.py:60
  3.6 6.9 %collective-permute-start.1 = (bf16[768,128]{1,0:T(8,128)(2,1)S(1)}, bf16[768,128]{1,0:T(8,128)(2,1)S(1)}, u32[]{:S(2)}, u32[]{:S(2)}) collective-permute-start(bf16[768,128]{1,0:T(8,128)(2,1)S(1)} %get-tuple-element.24), channel_id=1, source_target_pairs={{0,1},{2,3},{4,5},{6,7},{8,9},{10,11},{12,13},{14,15},{16,17},{18,... | collective-permute-start | bytes 589832 | tf_op jit(solution)/shard_map/ppermute | solution.py:60
  10.5 0.8 %copy-start = (f32[128,128]{1,0:T(8,128)S(1)}, f32[128,128]{1,0:T(8,128)}, u32[]{:S(2)}) copy-start(f32[128,128]{1,0:T(8,128)} %constant.2.clone.pow_ref) | copy-start | bytes 196612
  12.9 16.7 %collective-permute-start.2 = (s16[976,128]{1,0:T(8,128)(2,1)S(1)}, s16[976,128]{1,0:T(8,128)(2,1)S(1)}, u32[]{:S(2)}, u32[]{:S(2)}) collective-permute-start(s16[976,128]{1,0:T(8,128)(2,1)S(1)} %get-tuple-element.31), channel_id=1, source_target_pairs={{0,32},{32,64},{64,96},{96,128},{128,160},{160,192},{192,224},{1,3... | collective-permute-start | bytes 749576 | tf_op jit(solution)/shard_map/ppermute | solution.py:54
  15.6 12.9 %collective-permute-start.3 = (bf16[960,128]{1,0:T(8,128)(2,1)S(1)}, bf16[960,128]{1,0:T(8,128)(2,1)S(1)}, u32[]{:S(2)}, u32[]{:S(2)}) collective-permute-start(bf16[960,128]{1,0:T(8,128)(2,1)S(1)} %get-tuple-element.32), channel_id=1, source_target_pairs={{0,32},{32,64},{64,96},{96,128},{128,160},{160,192},{192,224},{224... | collective-permute-start | bytes 737288 | tf_op jit(solution)/shard_map/ppermute | solution.py:49
  16.4 4.0 %collective-permute-start.4 = (bf16[480,128]{1,0:T(8,128)(2,1)S(1)}, bf16[480,128]{1,0:T(8,128)(2,1)S(1)}, u32[]{:S(2)}, u32[]{:S(2)}) collective-permute-start(bf16[480,128]{1,0:T(8,128)(2,1)S(1)} %get-tuple-element.33), channel_id=1, source_target_pairs={{0,224},{32,0},{64,32},{96,64},{128,96},{160,128},{192,160},{224,1... | collective-permute-start | bytes 368648 | tf_op jit(solution)/shard_map/ppermute | solution.py:49
  18.4 2.1 %copy-start.2 = (s32[32]{0:T(128)S(1)}, s32[32]{0:T(128)}, u32[]{:S(2)}) copy-start(s32[32]{0:T(128)} %shift_ref.3) | copy-start | bytes 388
  18.4 2.1 %copy-start.3 = (s32[32]{0:T(128)S(1)}, s32[32]{0:T(128)}, u32[]{:S(2)}) copy-start(s32[32]{0:T(128)} %frac_ref.3) | copy-start | bytes 388
  18.4 2.1 %copy-start.4 = (f32[2]{0:T(128)S(1)}, f32[2]{0:T(128)}, u32[]{:S(2)}) copy-start(f32[2]{0:T(128)} %ext_ref.3) | copy-start | bytes 28
  28.5 1.2 %copy-start.1 = (f32[3,4]{1,0:T(4,128)S(1)}, f32[3,4]{1,0:T(4,128)}, u32[]{:S(2)}) copy-start(f32[3,4]{1,0:T(4,128)} %color_ref.1) | copy-start | bytes 148
  29.7 14.0 %copy-start.5 = (s32[32]{0:T(128)S(1)}, s32[32]{0:T(128)}, u32[]{:S(2)}) copy-start(s32[32]{0:T(128)} %rank_ref.1) | copy-start | bytes 388
